TPU v7x, 128 devices: a whole 4x4x4 slice. The times are simulated.
128 devices in a mesh: row: 8 (over y, core), col: 16 (over x, z).
Axes of the slice: x: 4, y: 4, z: 4, core: 2. Of those that a mesh axis runs over, the one named last changes fastest.
Arguments:
- fock_tiles: bfloat16 [1024, 15, 128, 128], P(('row', 'col')), may hold values from -6 to 6
- fock_pattern: int32 [1024, 15], replicated, may hold values from -1 to 1023, as said below
- basis_tiles: bfloat16 [1024, 15, 128, 128], P(('row', 'col')), may hold values from -0.25 to 0.25
- basis_pattern: int32 [1024, 15], replicated, may hold values from -1 to 1023, as said below
- product_pattern: int32 [1024, 15], replicated, may hold values from -1 to 1023, as said below
- result_pattern: int32 [1024, 15], replicated, may hold values from -1 to 1023, as said below
- new_index: int32 [1024], replicated, may hold values from 0 to 1023, as said below
Outputs:
- fock_orth: bfloat16 [1024, 15, 128, 128], P(('row', 'col'))
Inputs may be any that keep to these rules, and one draw needn't show every extreme that they name: `fock_pattern`: the filled slots of a tile row i come first and hold distinct tile columns within the (16) columns starting at min(max(i - 8, 0), 1008); slot 0 holds column i; from 10 to 15 slots of a row are filled, and the rest hold -1. `basis_pattern`: as for fock_pattern. `product_pattern`: as for fock_pattern. `result_pattern`: as for fock_pattern. `new_index`: A permutation; each tile row's new index lies in the same block of 128 consecutive tile rows and has the same remainder modulo 8; the 8 consecutive tile rows starting at a multiple of 8 move into 8 different blocks of 8 rows.
All inputs are finite; a program needn't handle non-finite values.
Results may differ from a plain program's by a relative error of at most 0.0065.
Values may be sent and summed in bfloat16 or wider, within the bound.
A program may use at most 192 MiB of HBM per device.

v0:
```python
import jax
import jax.numpy as jnp
from jax import lax
from jax.sharding import PartitionSpec as P

H = 8


def padded(block, sides, width):
    for axis, dim in sides:
        count = lax.axis_size(axis)
        forward = [(i, i + 1) for i in range(count - 1)]
        backward = [(target, source) for source, target in forward]
        low = lax.ppermute(
            lax.slice_in_dim(block, block.shape[dim] - width, None, axis=dim), axis, forward
        )
        high = lax.ppermute(lax.slice_in_dim(block, 0, width, axis=dim), axis, backward)
        block = jnp.concatenate([low, block, high], axis=dim)
    return block


def passed_along(array, axis, by):
    devices = lax.axis_size(axis)
    pairs = [(i, i + by) for i in range(devices) if 0 <= i + by < devices]
    return lax.ppermute(array, axis, pairs)


def body(
    fock_tiles, fock_pattern, basis_tiles, basis_pattern, product_pattern, result_pattern, new_index
):
    rows_dev = fock_tiles.shape[0]
    total_rows = fock_pattern.shape[0]
    reach = H
    near_count = rows_dev + 2 * reach
    device = lax.axis_index(("row", "col"))
    first_row = device * rows_dev
    near_start = first_row - reach
    fock_cols = lax.dynamic_slice_in_dim(fock_pattern, first_row, rows_dev, 0)
    prod_cols = lax.dynamic_slice_in_dim(product_pattern, first_row, rows_dev, 0)
    basis_cols = lax.dynamic_slice_in_dim(basis_pattern, first_row, rows_dev, 0)
    basis_near = padded(basis_tiles, ((("row", "col"), 0),), reach)

    def first_product(inputs):
        row_fock_cols, row_prod_cols, row_fock = inputs
        near_index = jnp.clip(row_fock_cols - near_start, 0, near_count - 1)
        gathered = basis_near[near_index]
        gathered_cols = basis_pattern[jnp.clip(row_fock_cols, 0, total_rows - 1)]
        match = (
            (gathered_cols[:, None, :] == row_prod_cols[None, :, None])
            & (row_prod_cols[None, :, None] >= 0)
            & (row_fock_cols[:, None, None] >= 0)
        )
        chosen = jnp.einsum(
            "kps,ksab->kpab",
            match.astype(jnp.bfloat16),
            gathered,
            preferred_element_type=jnp.float32,
        ).astype(jnp.bfloat16)
        return jnp.einsum(
            "kab,kpbc->pac", row_fock, chosen, preferred_element_type=jnp.float32
        ).astype(jnp.bfloat16)

    product = lax.map(first_product, (fock_cols, prod_cols, fock_tiles))

    def push_row(local_row, partial_value):
        row_tiles = lax.dynamic_index_in_dim(basis_tiles, local_row, 0, keepdims=False)
        row_product = lax.dynamic_index_in_dim(product, local_row, 0, keepdims=False)
        targets = lax.dynamic_index_in_dim(basis_cols, local_row, 0, keepdims=False)
        row_prod_cols = lax.dynamic_index_in_dim(prod_cols, local_row, 0, keepdims=False)
        valid = targets >= 0
        target_rows = jnp.clip(targets, 0, total_rows - 1)
        result_cols = result_pattern[target_rows]
        second = (
            (row_prod_cols[None, None, :] == result_cols[:, :, None])
            & (result_cols[:, :, None] >= 0)
            & valid[:, None, None]
        )
        picked = jnp.einsum(
            "srp,pab->srab",
            second.astype(jnp.bfloat16),
            row_product,
            preferred_element_type=jnp.float32,
        ).astype(jnp.bfloat16)
        terms = jnp.einsum("sba,srbc->srac", row_tiles, picked, preferred_element_type=jnp.float32)
        terms = terms * valid.astype(jnp.float32)[:, None, None, None]
        offsets = jnp.clip(target_rows - near_start, 0, near_count - 1)
        return partial_value.at[offsets].add(terms)

    partial_value = lax.fori_loop(
        0, rows_dev, push_row, jnp.zeros((near_count,) + fock_tiles.shape[1:], jnp.float32)
    )
    from_above = passed_along(
        partial_value[:reach].astype(jnp.bfloat16), ("row", "col"), -1
    ).astype(jnp.float32)
    from_below = passed_along(
        partial_value[rows_dev + reach :].astype(jnp.bfloat16), ("row", "col"), 1
    ).astype(jnp.float32)
    owned = partial_value[reach : reach + rows_dev]
    owned = owned.at[rows_dev - reach :].add(from_above)
    owned = owned.at[:reach].add(from_below)
    orth = owned.astype(jnp.bfloat16)
    width = lax.axis_size("col")
    own_new = lax.dynamic_slice_in_dim(new_index, first_row, rows_dev, 0)
    destinations = own_new // rows_dev % width
    select = destinations[None, :] == jnp.arange(width, dtype=jnp.int32)[:, None]
    source_slot = jnp.sum(
        select.astype(jnp.int32) * jnp.arange(rows_dev, dtype=jnp.int32)[None, :], axis=1
    )
    present = jnp.sum(select.astype(jnp.int32), axis=1) > 0
    outgoing = orth[source_slot] * present.astype(jnp.bfloat16)[:, None, None, None]
    incoming = lax.all_to_all(outgoing, "col", split_axis=0, concat_axis=0, tiled=True)
    wanted = first_row + jnp.arange(rows_dev, dtype=jnp.int32)
    found = new_index[None, :] == wanted[:, None]
    anchor = jnp.sum(
        found.astype(jnp.int32) * jnp.arange(total_rows, dtype=jnp.int32)[None, :], axis=1
    )
    anchor_col = anchor // rows_dev % width
    return incoming[anchor_col]


def solution(mesh):
    placed = (
        P(("row", "col"), None, None, None),
        P(),
        P(("row", "col"), None, None, None),
        P(),
        P(),
        P(),
        P(),
    )
    return jax.shard_map(
        body,
        mesh=mesh,
        in_specs=placed,
        out_specs=P(("row", "col"), None, None, None),
        check_vma=False,
    )
```

profile of v0, /device:TPU:8, one launch (start us, length us, event | category | flops | bytes accessed | tf_op | source)
XLA Modules:
  0.0 1066.3 jit_solution(2377630060101650944)
XLA Ops:
  12.9 80.3 %collective-permute-done = bf16[8,15,128,128]{3,2,1,0:T(8,128)(2,1)} collective-permute-done((bf16[8,15,128,128]{3,2,1,0:T(8,128)(2,1)}, bf16[8,15,128,128]{3,2,1,0:T(8,128)(2,1)}, u32[]{:S(2)}, u32[]{:S(2)}) %collective-permute-start) | collective-permute-done | bytes 3932192 | tf_op jit(solution)/shard_map/ppermute | solution.py:14
  95.7 10.2 pad_maximum_fusion
  105.9 180.1 %while.27 = (s32[]{:T(128)}, bf16[8,15,128,128]{2,3,1,0:T(8,128)(2,1)}, s32[8,15]{1,0:T(8,128)S(1)}, s32[1024,15]{1,0:T(8,128)S(1)}, s32[8,15]{1,0:T(8,128)S(1)}...) while((s32[]{:T(128)}, ...), condition=%wide.region_1.2_spmd, body=%wide.region_0.1_spmd.sunk | while | flops 1058254912 | bytes 37859784 | solution.py:63
  286.0 10.8 %broadcast_in_dim.33 = f32[24,15,128,128]{3,2,1,0:T(8,128)} broadcast(f32[]{:T(128)} %constant.202.clone.1), dimensions={} | broadcast | bytes 23592964 | tf_op jit(solution)/shard_map/broadcast_in_dim | solution.py:90
  296.8 492.7 %while.28 = (s32[]{:T(128)}, f32[24,15,128,128]{3,2,1,0:T(8,128)}, s32[8,15]{1,0:T(8,128)S(1)}, s32[]{:T(128)}, s32[8,15]{1,0:T(8,128)S(1)}, /*index=5*/s32[1024...) while((s32[]{:T(128)}, f32[24,15,128,128]{3,2,1,0:T(8,128)}, ...), condition=%wide.region_4.5_spmd, body=%wide.region_2.4_spmd.sunk | while | flops 1065381120 | bytes 106177840 | solution.py:89
  310.6 15.4 %copy.64 = f32[15,15,128,128]{3,2,1,0:T(8,128)} copy(f32[15,15,128,128]{2,3,1,0:T(8,128)} %multiply_bitcast_fusion.2) | data formatting | bytes 29491200 | tf_op jit(solution)/shard_map/while/body/eval_jaxpr/mul | solution.py:85
  326.0 32.3 %scatter_fusion = f32[24,15,128,128]{3,2,1,0:T(8,128)} fusion(f32[24,15,128,128]{3,2,1,0:T(8,128)} %get-tuple-element.479, s32[15]{0:T(128)S(1)} %get-tuple-element.438, f32[15,15,128,128]{3,2,1,0:T(8,128)} %copy.64), kind=kCustom, calls=%fused_computation.5.clone.1 | custom fusion | flops 3686400 | bytes 44236860 | tf_op jit(solution)/shard_map/while/body/eval_jaxpr/scatter-add | solution.py:87
  372.2 15.4 %copy.64 = f32[15,15,128,128]{3,2,1,0:T(8,128)} copy(f32[15,15,128,128]{2,3,1,0:T(8,128)} %multiply_bitcast_fusion.2) | data formatting | bytes 29491200 | tf_op jit(solution)/shard_map/while/body/eval_jaxpr/mul | solution.py:85
  387.6 32.3 %scatter_fusion = f32[24,15,128,128]{3,2,1,0:T(8,128)} fusion(f32[24,15,128,128]{3,2,1,0:T(8,128)} %get-tuple-element.479, s32[15]{0:T(128)S(1)} %get-tuple-element.438, f32[15,15,128,128]{3,2,1,0:T(8,128)} %copy.64), kind=kCustom, calls=%fused_computation.5.clone.1 | custom fusion | flops 3686400 | bytes 44236860 | tf_op jit(solution)/shard_map/while/body/eval_jaxpr/scatter-add | solution.py:87
  433.8 15.4 %copy.64 = f32[15,15,128,128]{3,2,1,0:T(8,128)} copy(f32[15,15,128,128]{2,3,1,0:T(8,128)} %multiply_bitcast_fusion.2) | data formatting | bytes 29491200 | tf_op jit(solution)/shard_map/while/body/eval_jaxpr/mul | solution.py:85
  449.2 32.3 %scatter_fusion = f32[24,15,128,128]{3,2,1,0:T(8,128)} fusion(f32[24,15,128,128]{3,2,1,0:T(8,128)} %get-tuple-element.479, s32[15]{0:T(128)S(1)} %get-tuple-element.438, f32[15,15,128,128]{3,2,1,0:T(8,128)} %copy.64), kind=kCustom, calls=%fused_computation.5.clone.1 | custom fusion | flops 3686400 | bytes 44236860 | tf_op jit(solution)/shard_map/while/body/eval_jaxpr/scatter-add | solution.py:87
  495.4 15.4 %copy.64 = f32[15,15,128,128]{3,2,1,0:T(8,128)} copy(f32[15,15,128,128]{2,3,1,0:T(8,128)} %multiply_bitcast_fusion.2) | data formatting | bytes 29491200 | tf_op jit(solution)/shard_map/while/body/eval_jaxpr/mul | solution.py:85
  510.8 32.5 %scatter_fusion = f32[24,15,128,128]{3,2,1,0:T(8,128)} fusion(f32[24,15,128,128]{3,2,1,0:T(8,128)} %get-tuple-element.479, s32[15]{0:T(128)S(1)} %get-tuple-element.438, f32[15,15,128,128]{3,2,1,0:T(8,128)} %copy.64), kind=kCustom, calls=%fused_computation.5.clone.1 | custom fusion | flops 3686400 | bytes 44236860 | tf_op jit(solution)/shard_map/while/body/eval_jaxpr/scatter-add | solution.py:87
  557.2 15.4 %copy.64 = f32[15,15,128,128]{3,2,1,0:T(8,128)} copy(f32[15,15,128,128]{2,3,1,0:T(8,128)} %multiply_bitcast_fusion.2) | data formatting | bytes 29491200 | tf_op jit(solution)/shard_map/while/body/eval_jaxpr/mul | solution.py:85
  572.6 32.3 %scatter_fusion = f32[24,15,128,128]{3,2,1,0:T(8,128)} fusion(f32[24,15,128,128]{3,2,1,0:T(8,128)} %get-tuple-element.479, s32[15]{0:T(128)S(1)} %get-tuple-element.438, f32[15,15,128,128]{3,2,1,0:T(8,128)} %copy.64), kind=kCustom, calls=%fused_computation.5.clone.1 | custom fusion | flops 3686400 | bytes 44236860 | tf_op jit(solution)/shard_map/while/body/eval_jaxpr/scatter-add | solution.py:87
  618.8 15.4 %copy.64 = f32[15,15,128,128]{3,2,1,0:T(8,128)} copy(f32[15,15,128,128]{2,3,1,0:T(8,128)} %multiply_bitcast_fusion.2) | data formatting | bytes 29491200 | tf_op jit(solution)/shard_map/while/body/eval_jaxpr/mul | solution.py:85
  634.2 32.3 %scatter_fusion = f32[24,15,128,128]{3,2,1,0:T(8,128)} fusion(f32[24,15,128,128]{3,2,1,0:T(8,128)} %get-tuple-element.479, s32[15]{0:T(128)S(1)} %get-tuple-element.438, f32[15,15,128,128]{3,2,1,0:T(8,128)} %copy.64), kind=kCustom, calls=%fused_computation.5.clone.1 | custom fusion | flops 3686400 | bytes 44236860 | tf_op jit(solution)/shard_map/while/body/eval_jaxpr/scatter-add | solution.py:87
  670.8 9.5 multiply_bitcast_fusion.2
  680.3 15.4 %copy.64 = f32[15,15,128,128]{3,2,1,0:T(8,128)} copy(f32[15,15,128,128]{2,3,1,0:T(8,128)} %multiply_bitcast_fusion.2) | data formatting | bytes 29491200 | tf_op jit(solution)/shard_map/while/body/eval_jaxpr/mul | solution.py:85
  695.7 32.3 %scatter_fusion = f32[24,15,128,128]{3,2,1,0:T(8,128)} fusion(f32[24,15,128,128]{3,2,1,0:T(8,128)} %get-tuple-element.479, s32[15]{0:T(128)S(1)} %get-tuple-element.438, f32[15,15,128,128]{3,2,1,0:T(8,128)} %copy.64), kind=kCustom, calls=%fused_computation.5.clone.1 | custom fusion | flops 3686400 | bytes 44236860 | tf_op jit(solution)/shard_map/while/body/eval_jaxpr/scatter-add | solution.py:87
  741.9 15.4 %copy.64 = f32[15,15,128,128]{3,2,1,0:T(8,128)} copy(f32[15,15,128,128]{2,3,1,0:T(8,128)} %multiply_bitcast_fusion.2) | data formatting | bytes 29491200 | tf_op jit(solution)/shard_map/while/body/eval_jaxpr/mul | solution.py:85
  757.3 32.2 %scatter_fusion = f32[24,15,128,128]{3,2,1,0:T(8,128)} fusion(f32[24,15,128,128]{3,2,1,0:T(8,128)} %get-tuple-element.479, s32[15]{0:T(128)S(1)} %get-tuple-element.438, f32[15,15,128,128]{3,2,1,0:T(8,128)} %copy.64), kind=kCustom, calls=%fused_computation.5.clone.1 | custom fusion | flops 3686400 | bytes 44236860 | tf_op jit(solution)/shard_map/while/body/eval_jaxpr/scatter-add | solution.py:87
  807.2 79.5 %collective-permute-done.2 = bf16[8,15,128,128]{3,2,1,0:T(8,128)(2,1)S(1)} collective-permute-done((bf16[8,15,128,128]{3,2,1,0:T(8,128)(2,1)S(1)}, bf16[8,15,128,128]{3,2,1,0:T(8,128)(2,1)S(1)}, u32[]{:S(2)}, u32[]{:S(2)}) %collective-permute-start.2) | collective-permute-done | bytes 3932192 | tf_op jit(solution)/shard_map/ppermute | solution.py:25
  920.2 139.9 %all-to-all-done = bf16[16,15,128,128]{3,2,1,0:T(8,128)(2,1)} async-done(((bf16[16,15,128,128]{3,2,1,0:T(8,128)(2,1)}), bf16[16,15,128,128]{3,2,1,0:T(8,128)(2,1)}, u32[]{:S(2)}, u32[]{:S(2)}) %all-to-all-start) | async-done | bytes 7864352 | tf_op jit(solution)/shard_map/all_to_all | solution.py:111
  (174 shorter events, 353.6 us)
Async XLA Ops:
  0.0 93.2 %collective-permute-start = (bf16[8,15,128,128]{3,2,1,0:T(8,128)(2,1)}, bf16[8,15,128,128]{3,2,1,0:T(8,128)(2,1)}, u32[]{:S(2)}, u32[]{:S(2)}) collective-permute-start(bf16[8,15,128,128]{3,2,1,0:T(8,128)(2,1)} %param.21), channel_id=1, source_target_pairs={{0,1},{1,2},{2,3},{3,4},{4,5},{5,6},{6,7},{7,8},{8,9},{9,10},{10,1... | collective-permute-start | bytes 11796488 | tf_op jit(solution)/shard_map/ppermute | solution.py:14
  3.8 91.9 %collective-permute-start.1 = (bf16[8,15,128,128]{3,2,1,0:T(8,128)(2,1)}, bf16[8,15,128,128]{3,2,1,0:T(8,128)(2,1)}, u32[]{:S(2)}, u32[]{:S(2)}) collective-permute-start(bf16[8,15,128,128]{3,2,1,0:T(8,128)(2,1)} %param.21), channel_id=1, source_target_pairs={{1,0},{2,1},{3,2},{4,3},{5,4},{6,5},{7,6},{8,7},{9,8},{10,9},{11,1... | collective-permute-start | bytes 11796488 | tf_op jit(solution)/shard_map/ppermute | solution.py:17
  798.6 8.4 copy-start
  799.7 87.0 %collective-permute-start.2 = (bf16[8,15,128,128]{3,2,1,0:T(8,128)(2,1)S(1)}, bf16[8,15,128,128]{3,2,1,0:T(8,128)(2,1)S(1)}, u32[]{:S(2)}, u32[]{:S(2)}) collective-permute-start(bf16[8,15,128,128]{3,2,1,0:T(8,128)(2,1)S(1)} %get-tuple-element.320), channel_id=1, source_target_pairs={{1,0},{2,1},{3,2},{4,3},{5,4},{6,5},{7,6},{8,7},{9,8},{10,9},{11,1... | collective-permute-start | bytes 11796488 | tf_op jit(solution)/shard_map/ppermute | solution.py:25
  805.1 89.2 %collective-permute-start.3 = (bf16[8,15,128,128]{3,2,1,0:T(8,128)(2,1)S(1)}, bf16[8,15,128,128]{3,2,1,0:T(8,128)(2,1)S(1)}, u32[]{:S(2)}, u32[]{:S(2)}) collective-permute-start(bf16[8,15,128,128]{3,2,1,0:T(8,128)(2,1)S(1)} %get-tuple-element.321), channel_id=1, source_target_pairs={{0,1},{1,2},{2,3},{3,4},{4,5},{5,6},{6,7},{7,8},{8,9},{9,10},{10,1... | collective-permute-start | bytes 11796488 | tf_op jit(solution)/shard_map/ppermute | solution.py:25
  915.3 144.9 %all-to-all-start = ((bf16[16,15,128,128]{3,2,1,0:T(8,128)(2,1)}), bf16[16,15,128,128]{3,2,1,0:T(8,128)(2,1)}, u32[]{:S(2)}, u32[]{:S(2)}) async-start(bf16[16,15,128,128]{3,2,1,0:T(8,128)(2,1)} %broadcast_multiply_fusion), calls=%async_computation | async-start | bytes 15728640 | tf_op jit(solution)/shard_map/all_to_all | solution.py:111
where the time goes:
time: 1080 us; the launch traced here: 1070 us
  waiting for transfers between devices  310 us (29%)
  other arithmetic  293 us (27%)
  local copies, waits for them, and re-layouts  243 us (22%)
  matrix products  198 us (18%)
  starting transfers between devices  21.8 us (2%)
    scatter-add x8, other arithmetic, push_row(): return partial_value.at[offsets].add(terms)  259 us
    all_to_all x1, waiting for transfers between devices, body(): lax.all_to_all(outgoing, 'col', split_axis=0, concat_axis=0, tiled=True)  140 us
    mul x8, local copies, waits for them, and re-layouts, push_row(): terms = terms * valid.astype(jnp.float32)[:, None, None, None]  123 us
    ppermute x2, waiting for transfers between devices, passed_along(): return lax.ppermute(array, axis, pairs)  87.1 us
    ppermute x1, waiting for transfers between devices, padded(): lax.ppermute(lax.slice_in_dim(block, block.shape[dim] - width, None, axis...  80.3 us
    dot_general x8, matrix products, push_row(): jnp.einsum('sba,srbc->srac', row_tiles, picked, preferred_element_type=jn...  75.8 us
    gather x8, local copies, waits for them, and re-layouts, first_product(): gathered = basis_near[near_index]  70.8 us
    dot_general x8, matrix products, first_product(): jnp.einsum('kps,ksab->kpab', match.astype(jnp.bfloat16), gathered, prefer...  64.7 us
  transfers between devices with their start and end apart: 5, of which 5 were waited for; matrix products, arithmetic and copies ran while one was open for 0% of the time, Pallas kernels for 0%

commit v1 on v0

v1 whole, which is shorter than its diff:
```python
import functools

import jax
import jax.numpy as jnp
from jax import lax
from jax.experimental import pallas as pl
from jax.experimental.pallas import tpu as pltpu
from jax.sharding import PartitionSpec as P

T = 128
R = 8
K = 15
C = 24
TRI = R * (R + 1) // 2
PACK = R * R + TRI - R
VMEM_LIMIT = 60 * 1024 * 1024
BF = jnp.bfloat16
ANY = pl.BlockSpec(memory_space=pl.ANY)
SMEM = pl.BlockSpec(memory_space=pltpu.SMEM)


def up_pieces():
    pieces, off = [], 0
    for col in range(8, 16):
        pieces.append((col, 0, 8, off))
        off += 8
    for u in range(7):
        pieces.append((16 + u, u + 1, 7 - u, off))
        off += 7 - u
    return pieces


def down_pieces():
    pieces, off = [], 0
    for u in range(8):
        pieces.append((u, 0, u + 1, off))
        off += u + 1
    for col in range(8, 15):
        pieces.append((col, 0, 8, off))
        off += 8
    return pieces


def first_pieces():
    pieces, off = [], 0
    for u in range(8):
        pieces.append((16 + u, 0, u + 1, off))
        off += u + 1
    return pieces


def last_pieces():
    pieces, off = [], 0
    for u in range(7):
        pieces.append((u, u + 1, 7 - u, off))
        off += 7 - u
    return pieces


def second_pieces():
    return [(15, 0, 8, 0)]


def run_all(copies):
    for copy in copies:
        copy.start()
    for copy in copies:
        copy.wait()


def send_copies(buf, out, pieces, sem):
    return [
        pltpu.make_async_copy(buf.at[col, pl.ds(row, rows)], out.at[pl.ds(off, rows)], sem)
        for col, row, rows, off in pieces
    ]


def pack_out(device, last, buf, up, down, ext, sem):
    run_all(
        send_copies(buf, up, up_pieces(), sem) + send_copies(buf, down, down_pieces(), sem)
    )
    for which, pieces in ((0, first_pieces()), (1, second_pieces()), (last, last_pieces())):

        @pl.when(device == which)
        def _():
            run_all(send_copies(buf, ext, pieces, sem))


def scatter_start(rel, tiles, dst, base, sem):
    def row(t, carry):
        def slot(s, inner):
            col = rel[t, s]

            @pl.when(col >= 0)
            def _():
                pltpu.make_async_copy(tiles.at[t, s], dst.at[col, base + t], sem).start()

            return inner

        return lax.fori_loop(0, K, slot, carry)

    lax.fori_loop(0, R, row, 0)


def scatter_wait(rel, tiles, dst, base, sem):
    def row(t, carry):
        def slot(s, inner):
            @pl.when(rel[t, s] >= 0)
            def _():
                pltpu.make_async_copy(tiles.at[t, s], dst.at[0, base + t], sem).wait()

            return inner

        return lax.fori_loop(0, K, slot, carry)

    lax.fori_loop(0, R, row, 0)


def zero_block(ref, lead):
    def one(q, carry):
        ref[q] = jnp.zeros(ref.shape[1:], ref.dtype)
        return carry

    lax.fori_loop(0, lead, one, 0)


def pack_kernel(last, info, zrel, z, up, down, ext, buf, sem):
    zero_block(buf, C)
    scatter_start(zrel, z, buf, 0, sem)
    scatter_wait(zrel, z, buf, 0, sem)
    pack_out(info[0], last, buf, up, down, ext, sem)


def window_copies(win, low, high, sem):
    copies = []
    for col, row, rows, off in up_pieces():
        copies.append(
            pltpu.make_async_copy(low.at[pl.ds(off, rows)], win.at[col - 8, pl.ds(row, rows)], sem)
        )
    for col, row, rows, off in down_pieces():
        copies.append(
            pltpu.make_async_copy(
                high.at[pl.ds(off, rows)], win.at[col + 8, pl.ds(16 + row, rows)], sem
            )
        )
    return copies


def zero_gaps(win):
    def corner(q, carry):
        win[16 + q, pl.ds(0, 8)] = jnp.zeros((8, T, T), BF)
        win[q, pl.ds(16, 8)] = jnp.zeros((8, T, T), BF)
        return carry

    lax.fori_loop(0, 8, corner, 0)
    for u in range(8):
        win[8 + u, pl.ds(0, u + 1)] = jnp.zeros((u + 1, T, T), BF)
        if u < 7:
            win[8 + u, pl.ds(17 + u, 7 - u)] = jnp.zeros((7 - u, T, T), BF)
    win[23, pl.ds(16, 8)] = jnp.zeros((8, T, T), BF)


def edge_window(device, last, win, ext, sem):
    def fill(which, pieces, shift, base):
        @pl.when(device == which)
        def _():
            run_all(
                [
                    pltpu.make_async_copy(
                        ext.at[pl.ds(off, rows)], win.at[col + shift, pl.ds(base + row, rows)], sem
                    )
                    for col, row, rows, off in pieces
                ]
            )

    fill(1, first_pieces(), -8, 0)
    fill(0, second_pieces(), 8, 16)
    fill(last - 1, last_pieces(), 8, 16)


def band_step(left, win, pair, rows, start, depth, put):
    lhs = jnp.concatenate(
        [left[start + q, pl.ds(2 * rows, 2)].reshape(2 * T, T) for q in range(depth)], axis=1
    )
    rhs = jnp.concatenate(
        [win[2 * pair + h, pl.ds(start, depth)].reshape(depth * T, T) for h in range(2)], axis=1
    )
    total = jnp.dot(lhs, rhs, preferred_element_type=jnp.float32)
    for h in range(2):
        for m in range(2):
            put(2 * pair + h, 2 * rows + m, total[m * T : (m + 1) * T, h * T : (h + 1) * T])


def band_product(edge, left, win, put):
    @pl.when(edge == 0)
    def _():
        def pair_step(pair, carry):
            start = jnp.minimum(jnp.maximum(2 * pair - 8, 0), 6)
            low = jnp.maximum(pair - 8, 0)
            high = jnp.minimum(pair, 3)

            def rows_step(rows, inner):
                band_step(left, win, pair, rows, start, 18, put)
                return inner

            return lax.fori_loop(low, high + 1, rows_step, carry)

        lax.fori_loop(0, C // 2, pair_step, 0)

    @pl.when(edge != 0)
    def _():
        def step(q, carry):
            band_step(left, win, q // 4, lax.rem(q, 4), 0, C, put)
            return carry

        lax.fori_loop(0, C // 2 * 4, step, 0)


def first_kernel(
    last, info, zrel, frel, keep, z, f, low, high, ext,
    prod, up, down, pext, zwin, win, left, out, sem, sem2, sem3,
):
    device = info[0]
    copies = window_copies(win, low, high, sem)
    for copy in copies:
        copy.start()
    zero_gaps(win)

    def own(q, carry):
        win[q, pl.ds(8, 8)] = jnp.zeros((8, T, T), BF)
        return carry

    lax.fori_loop(0, C, own, 0)
    zero_block(left, C)
    scatter_start(zrel, z, win, 8, sem2)
    scatter_start(frel, f, left, 0, sem3)
    zero_block(out, C)
    for copy in copies:
        copy.wait()
    edge_window(device, last, win, ext, sem)
    scatter_wait(zrel, z, win, 8, sem2)
    scatter_wait(frel, f, left, 0, sem3)
    keep_win = pltpu.make_async_copy(win.at[pl.ds(8, 8)], zwin, sem)
    keep_win.start()

    def put(col, row, value):
        out[col, row] = jnp.where(keep[col, row] > 0, value, 0.0).astype(BF)

    band_product(info[1], left, win, put)
    keep_win.wait()
    whole = pltpu.make_async_copy(out, prod, sem2)
    whole.start()
    pack_out(device, last, out, up, down, pext, sem)
    whole.wait()


def turn_kernel(zwin, turned):
    for a in range(R):
        turned[0, a] = zwin[a, 0].T


def second_kernel(
    last, info, rrel, dest, prod, turned, low, high, ext, outgoing, win, left, out, sem, sem2
):
    copies = window_copies(win, low, high, sem)
    copies.append(pltpu.make_async_copy(prod, win.at[:, pl.ds(8, 8)], sem))
    copies.append(pltpu.make_async_copy(turned, left, sem))
    for copy in copies:
        copy.start()
    zero_gaps(win)
    zero_block(out, C + 1)
    for copy in copies:
        copy.wait()
    edge_window(info[0], last, win, ext, sem)

    def put(col, row, value):
        out[col, row] = value.astype(BF)

    band_product(info[1], left, win, put)

    def deliver(go):
        def row(t, carry):
            def slot(s, inner):
                copy = pltpu.make_async_copy(
                    out.at[rrel[t, s], t], outgoing.at[dest[t], s], sem2
                )
                copy.start() if go else copy.wait()
                return inner

            return lax.fori_loop(0, K, slot, carry)

        lax.fori_loop(0, R, row, 0)

    deliver(True)
    deliver(False)


def take_kernel(source, incoming, out):
    out[...] = incoming[...]


def tiles(count):
    return jax.ShapeDtypeStruct((count, T, T), BF)


def body(
    fock_tiles, fock_pattern, basis_tiles, basis_pattern, product_pattern, result_pattern, new_index
):
    total_rows = fock_pattern.shape[0]
    width = lax.axis_size("col")
    devices = lax.axis_size("row") * width
    last = devices - 1
    device = lax.axis_index(("row", "col"))
    first_row = device * R
    params = pltpu.CompilerParams(vmem_limit_bytes=VMEM_LIMIT)

    def relative(pattern, empty):
        own = lax.dynamic_slice_in_dim(pattern, first_row, R, 0)
        return jnp.where(own >= 0, own - first_row + 8, empty)

    zrel = relative(basis_pattern, -1)
    frel = relative(fock_pattern, -1)
    prel = relative(product_pattern, -1)
    rrel = relative(result_pattern, C)
    keep = jnp.any(
        prel[None] == jnp.arange(C, dtype=jnp.int32)[:, None, None], axis=-1
    ).astype(jnp.int32)
    edge = ((device < 2) | (device > last - 2)).astype(jnp.int32)
    info = jnp.stack([device.astype(jnp.int32), edge])

    axes = ("row", "col")
    rise = [(q, q + 1) for q in range(devices - 1)]
    fall = [(q + 1, q) for q in range(devices - 1)]
    ends = [(0, 1), (1, 0), (last, last - 1)]

    up, down, ext = pl.pallas_call(
        functools.partial(pack_kernel, last),
        out_shape=(tiles(PACK), tiles(PACK), tiles(TRI)),
        in_specs=[SMEM, SMEM, ANY],
        out_specs=(ANY, ANY, ANY),
        scratch_shapes=[pltpu.VMEM((C, R, T, T), BF), pltpu.SemaphoreType.DMA],
        compiler_params=params,
        name="pack",
    )(info, zrel, basis_tiles)
    low = lax.ppermute(up, axes, rise)
    high = lax.ppermute(down, axes, fall)
    ext = lax.ppermute(ext, axes, ends)

    block = jax.ShapeDtypeStruct((C, R, T, T), BF)
    prod, up, down, pext, zwin = pl.pallas_call(
        functools.partial(first_kernel, last),
        out_shape=(
            block, tiles(PACK), tiles(PACK), tiles(TRI), jax.ShapeDtypeStruct((R, C, T, T), BF)
        ),
        in_specs=[SMEM] * 4 + [ANY] * 5,
        out_specs=(ANY,) * 5,
        scratch_shapes=[
            pltpu.VMEM((C, C, T, T), BF),
            pltpu.VMEM((C, R, T, T), BF),
            pltpu.VMEM((C, R, T, T), BF),
            pltpu.SemaphoreType.DMA,
            pltpu.SemaphoreType.DMA,
            pltpu.SemaphoreType.DMA,
        ],
        compiler_params=params,
        name="first",
    )(info, zrel, frel, keep, basis_tiles, fock_tiles, low, high, ext)
    low = lax.ppermute(up, axes, rise)
    high = lax.ppermute(down, axes, fall)
    pext = lax.ppermute(pext, axes, ends)
    turned = pl.pallas_call(
        turn_kernel,
        grid=(C,),
        out_shape=block,
        in_specs=[pl.BlockSpec((R, 1, T, T), lambda q: (0, q, 0, 0))],
        out_specs=pl.BlockSpec((1, R, T, T), lambda q: (q, 0, 0, 0)),
        cost_estimate=pl.CostEstimate(
            flops=1, bytes_accessed=4 * C * R * T * T, transcendentals=0
        ),
        name="turn",
    )(zwin)

    own_new = lax.dynamic_slice_in_dim(new_index, first_row, R, 0)
    dest = own_new // R % width
    outgoing = pl.pallas_call(
        functools.partial(second_kernel, last),
        out_shape=jax.ShapeDtypeStruct((width, K, T, T), BF),
        in_specs=[SMEM] * 3 + [ANY] * 5,
        out_specs=ANY,
        scratch_shapes=[
            pltpu.VMEM((C, C, T, T), BF),
            pltpu.VMEM((C, R, T, T), BF),
            pltpu.VMEM((C + 1, R, T, T), BF),
            pltpu.SemaphoreType.DMA,
            pltpu.SemaphoreType.DMA,
        ],
        compiler_params=params,
        name="second",
    )(info, rrel, dest, prod, turned, low, high, pext)

    incoming = lax.all_to_all(outgoing, "col", split_axis=0, concat_axis=0, tiled=True)
    wanted = first_row + jnp.arange(R, dtype=jnp.int32)
    found = new_index[None, :] == wanted[:, None]
    anchor = jnp.sum(
        jnp.where(found, jnp.arange(total_rows, dtype=jnp.int32)[None, :], 0), axis=1
    )
    source = anchor // R % width
    return pl.pallas_call(
        take_kernel,
        grid_spec=pltpu.PrefetchScalarGridSpec(
            num_scalar_prefetch=1,
            grid=(R,),
            in_specs=[pl.BlockSpec((1, K, T, T), lambda q, s: (s[q], 0, 0, 0))],
            out_specs=pl.BlockSpec((1, K, T, T), lambda q, s: (q, 0, 0, 0)),
        ),
        out_shape=jax.ShapeDtypeStruct((R, K, T, T), BF),
        name="take",
    )(source, incoming)


def solution(mesh):
    placed = (
        P(("row", "col"), None, None, None),
        P(),
        P(("row", "col"), None, None, None),
        P(),
        P(),
        P(),
        P(),
    )
    return jax.shard_map(
        body,
        mesh=mesh,
        in_specs=placed,
        out_specs=P(("row", "col"), None, None, None),
        check_vma=False,
    )
```

time: 1080 us -> 379 us (0.35)
  the two profiles are of different devices: /device:TPU:8 before, /device:TPU:77 now
where the time goes in v1:
time: 379 us; the launch traced here: 378 us
  waiting for transfers between devices  253 us (67%)
  Pallas kernels  87.5 us (23%)
  starting transfers between devices  29.5 us (8%)
  other arithmetic  3.94 us (1%)
    all_to_all x1, waiting for transfers between devices, body(): lax.all_to_all(outgoing, 'col', split_axis=0, concat_axis=0, tiled=True)  144 us
    ppermute x2, waiting for transfers between devices, body(): low = lax.ppermute(up, axes, rise)  102 us
    pallas_call x1, Pallas kernels, body(): pl.pallas_call(functools.partial(first_kernel, last), out_shape=(block, t...  31.5 us
    pallas_call x1, Pallas kernels, body(): pl.pallas_call(functools.partial(second_kernel, last), out_shape=jax.Shap...  26.5 us
    pallas_call x1, Pallas kernels, body(): pl.pallas_call(turn_kernel, grid=(C,), out_shape=block, in_specs=[pl.Bloc...  15.7 us
    all_to_all x1, starting transfers between devices, body(): lax.all_to_all(outgoing, 'col', split_axis=0, concat_axis=0, tiled=True)  14.5 us
  transfers between devices with their start and end apart: 7, of which 5 were waited for; matrix products, arithmetic and copies ran while one was open for 1% of the time, Pallas kernels for 4%

profile of v1, /device:TPU:77, one launch (start us, length us, event | category | flops | bytes accessed | tf_op | source)
XLA Modules:
  0.0 377.5 jit_solution(11525086061486266722)
XLA Ops:
  0.0 0.8 copy-done
  1.0 0.8 constant_dynamic-slice_fusion
  1.8 0.6 pad_add_fusion.info
  3.1 6.7 %pack.1 = (bf16[92,128,128]{2,1,0:T(8,128)(2,1)}, bf16[92,128,128]{2,1,0:T(8,128)(2,1)}, bf16[36,128,128]{2,1,0:T(8,128)(2,1)}) custom-call(s32[2]{0:T(128)} %pad_add_fusion.info, s32[8,15]{1,0:T(8,128)} %get-tuple-element.22.zrel, bf16[8,15,128,128]{3,2,1,0:T(8,128)(2,1)} %z.3), custom_call_target="tpu_custom_call" | custom-call | tf_op jit(solution)/shard_map/pack/pallas_call | solution.py:336
  9.8 3.3 collective-permute-start
  13.1 2.0 collective-permute-start.1
  15.1 1.7 collective-permute-start.2
  17.0 0.7 copy.23.keep
  17.7 0.8 constant_dynamic-slice_fusion.1
  18.5 0.6 add_select_fusion.1.frel
  19.1 59.0 %collective-permute-done.low = bf16[92,128,128]{2,1,0:T(8,128)(2,1)S(1)} collective-permute-done((bf16[92,128,128]{2,1,0:T(8,128)(2,1)}, bf16[92,128,128]{2,1,0:T(8,128)(2,1)S(1)}, u32[]{:S(2)}, u32[]{:S(2)}) %collective-permute-start) | collective-permute-done | bytes 3014688 | tf_op jit(solution)/shard_map/ppermute | solution.py:345
  78.2 3.0 collective-permute-done.1.high
  81.2 31.5 %first.1 = (bf16[24,8,128,128]{3,2,1,0:T(8,128)(2,1)}, bf16[92,128,128]{2,1,0:T(8,128)(2,1)}, bf16[92,128,128]{2,1,0:T(8,128)(2,1)}, bf16[36,128,128]{2,1,0:T(8,128)(2,1)}, bf16[8,24,128,128]{3,2,1,0:T(8,128)(2,1)}) custom-call(s32[2]{0:T(128)} %pad_add_fusion.info, s32[8,15]{1,0:T(8,128)} %get-tuple-element.22.zrel, s32[8,15]{1,0:T(8,128)} %add_select_fusion.1.frel, ...), custom_call_target="tpu_custom_call" | custom-call | tf_op jit(solution)/shard_map/first/pallas_call | solution.py:350
  112.7 4.3 %collective-permute-start.3 = (bf16[92,128,128]{2,1,0:T(8,128)(2,1)}, bf16[92,128,128]{2,1,0:T(8,128)(2,1)S(1)}, u32[]{:S(2)}, u32[]{:S(2)}) collective-permute-start(bf16[92,128,128]{2,1,0:T(8,128)(2,1)} %get-tuple-element.18), channel_id=1, source_target_pairs={{0,1},{1,2},{2,3},{3,4},{4,5},{5,6},{6,7},{7,8},{8,9},{9,10},{10,1... | collective-permute-start | bytes 9043976 | tf_op jit(solution)/shard_map/ppermute | solution.py:368
  117.0 1.9 collective-permute-start.4
  118.9 1.8 collective-permute-start.5
  120.8 0.6 and_select_fusion.dest
  122.0 15.7 %turn.1.turned = bf16[24,8,128,128]{3,2,1,0:T(8,128)(2,1)} custom-call(bf16[8,24,128,128]{3,2,1,0:T(8,128)(2,1)} %get-tuple-element.17.zwin), custom_call_target="tpu_custom_call" | custom-call | flops 1 | bytes 12582912 | tf_op jit(solution)/shard_map/turn/pallas_call | solution.py:371
  137.7 42.7 %collective-permute-done.3.low = bf16[92,128,128]{2,1,0:T(8,128)(2,1)S(1)} collective-permute-done((bf16[92,128,128]{2,1,0:T(8,128)(2,1)}, bf16[92,128,128]{2,1,0:T(8,128)(2,1)S(1)}, u32[]{:S(2)}, u32[]{:S(2)}) %collective-permute-start.3) | collective-permute-done | bytes 3014688 | tf_op jit(solution)/shard_map/ppermute | solution.py:368
  180.4 3.8 %collective-permute-done.4.high = bf16[92,128,128]{2,1,0:T(8,128)(2,1)} collective-permute-done((bf16[92,128,128]{2,1,0:T(8,128)(2,1)}, bf16[92,128,128]{2,1,0:T(8,128)(2,1)}, u32[]{:S(2)}, u32[]{:S(2)}) %collective-permute-start.4) | collective-permute-done | bytes 3014688 | tf_op jit(solution)/shard_map/ppermute | solution.py:369
  184.3 26.5 %second.1 = bf16[16,15,128,128]{3,2,1,0:T(8,128)(2,1)} custom-call(s32[2]{0:T(128)} %pad_add_fusion.info, s32[8,15]{1,0:T(8,128)} %add_select_fusion.3.rrel, s32[8]{0:T(128)} %and_select_fusion.dest, bf16[24,8,128,128]{3,2,1,0:T(8,128)(2,1)} %get-tuple-element.16.prod, bf16[24,8,128,128]{3,2,1,0:T(8,128)(2,1)} %turn.1.turned, ...), custom_call_target="tpu_custom_call" | custom-call | tf_op jit(solution)/shard_map/second/pallas_call | solution.py:385
  210.7 14.5 %all-to-all-start = ((bf16[16,15,128,128]{3,2,1,0:T(8,128)(2,1)}), bf16[16,15,128,128]{3,2,1,0:T(8,128)(2,1)}, u32[]{:S(2)}, u32[]{:S(2)}) async-start(bf16[16,15,128,128]{3,2,1,0:T(8,128)(2,1)} %second.1), calls=%async_computation | async-start | bytes 15728640 | tf_op jit(solution)/shard_map/all_to_all | solution.py:401
  226.0 144.3 %all-to-all-done.incoming = bf16[16,15,128,128]{3,2,1,0:T(8,128)(2,1)} async-done(((bf16[16,15,128,128]{3,2,1,0:T(8,128)(2,1)}), bf16[16,15,128,128]{3,2,1,0:T(8,128)(2,1)}, u32[]{:S(2)}, u32[]{:S(2)}) %all-to-all-start) | async-done | bytes 7864352 | tf_op jit(solution)/shard_map/all_to_all | solution.py:401
  370.3 7.2 %take.1 = bf16[8,15,128,128]{3,2,1,0:T(8,128)(2,1)} custom-call(s32[8]{0:T(128)} %and_select_fusion.2.source, bf16[16,15,128,128]{3,2,1,0:T(8,128)(2,1)} %all-to-all-done.incoming), custom_call_target="tpu_custom_call" | custom-call | tf_op jit(solution)/shard_map/take/pallas_call | solution.py:408
  (24 shorter events, 2.6 us)
Async XLA Ops:
  0.0 0.8 copy-start
  9.8 68.4 %collective-permute-start = (bf16[92,128,128]{2,1,0:T(8,128)(2,1)}, bf16[92,128,128]{2,1,0:T(8,128)(2,1)S(1)}, u32[]{:S(2)}, u32[]{:S(2)}) collective-permute-start(bf16[92,128,128]{2,1,0:T(8,128)(2,1)} %get-tuple-element.13), channel_id=1, source_target_pairs={{0,1},{1,2},{2,3},{3,4},{4,5},{5,6},{6,7},{7,8},{8,9},{9,10},{10,1... | collective-permute-start | bytes 9043976 | tf_op jit(solution)/shard_map/ppermute | solution.py:345
  13.1 68.1 %collective-permute-start.1 = (bf16[92,128,128]{2,1,0:T(8,128)(2,1)}, bf16[92,128,128]{2,1,0:T(8,128)(2,1)}, u32[]{:S(2)}, u32[]{:S(2)}) collective-permute-start(bf16[92,128,128]{2,1,0:T(8,128)(2,1)} %get-tuple-element.14), channel_id=1, source_target_pairs={{1,0},{2,1},{3,2},{4,3},{5,4},{6,5},{7,6},{8,7},{9,8},{10,9},{11,1... | collective-permute-start | bytes 9043976 | tf_op jit(solution)/shard_map/ppermute | solution.py:346
  15.1 4.0 %collective-permute-start.2 = (bf16[36,128,128]{2,1,0:T(8,128)(2,1)}, bf16[36,128,128]{2,1,0:T(8,128)(2,1)}, u32[]{:S(2)}, u32[]{:S(2)}) collective-permute-start(bf16[36,128,128]{2,1,0:T(8,128)(2,1)} %get-tuple-element.15), channel_id=1, source_target_pairs={{0,1},{1,0},{127,126}} | collective-permute-start | bytes 3538952 | tf_op jit(solution)/shard_map/ppermute | solution.py:347
  19.1 101.6 %copy-start.4 = (s32[1024]{0:T(1024)S(1)}, s32[1024]{0:T(1024)}, u32[]{:S(2)}) copy-start(s32[1024]{0:T(1024)} %param.13) | copy-start | bytes 12292
  78.2 3.0 copy-start.2
  112.7 67.7 %collective-permute-start.3 = (bf16[92,128,128]{2,1,0:T(8,128)(2,1)}, bf16[92,128,128]{2,1,0:T(8,128)(2,1)S(1)}, u32[]{:S(2)}, u32[]{:S(2)}) collective-permute-start(bf16[92,128,128]{2,1,0:T(8,128)(2,1)} %get-tuple-element.18), channel_id=1, source_target_pairs={{0,1},{1,2},{2,3},{3,4},{4,5},{5,6},{6,7},{7,8},{8,9},{9,10},{10,1... | collective-permute-start | bytes 9043976 | tf_op jit(solution)/shard_map/ppermute | solution.py:368
  117.0 67.2 %collective-permute-start.4 = (bf16[92,128,128]{2,1,0:T(8,128)(2,1)}, bf16[92,128,128]{2,1,0:T(8,128)(2,1)}, u32[]{:S(2)}, u32[]{:S(2)}) collective-permute-start(bf16[92,128,128]{2,1,0:T(8,128)(2,1)} %get-tuple-element.19), channel_id=1, source_target_pairs={{1,0},{2,1},{3,2},{4,3},{5,4},{6,5},{7,6},{8,7},{9,8},{10,9},{11,1... | collective-permute-start | bytes 9043976 | tf_op jit(solution)/shard_map/ppermute | solution.py:369
  118.9 18.7 %collective-permute-start.5 = (bf16[36,128,128]{2,1,0:T(8,128)(2,1)}, bf16[36,128,128]{2,1,0:T(8,128)(2,1)}, u32[]{:S(2)}, u32[]{:S(2)}) collective-permute-start(bf16[36,128,128]{2,1,0:T(8,128)(2,1)} %get-tuple-element.20), channel_id=1, source_target_pairs={{0,1},{1,0},{127,126}} | collective-permute-start | bytes 3538952 | tf_op jit(solution)/shard_map/ppermute | solution.py:370
  180.4 3.8 %copy-start.3 = (bf16[92,128,128]{2,1,0:T(8,128)(2,1)}, bf16[92,128,128]{2,1,0:T(8,128)(2,1)S(1)}, u32[]{:S(2)}) copy-start(bf16[92,128,128]{2,1,0:T(8,128)(2,1)S(1)} %collective-permute-done.3.low) | copy-start | bytes 9043972
  210.7 159.6 %all-to-all-start = ((bf16[16,15,128,128]{3,2,1,0:T(8,128)(2,1)}), bf16[16,15,128,128]{3,2,1,0:T(8,128)(2,1)}, u32[]{:S(2)}, u32[]{:S(2)}) async-start(bf16[16,15,128,128]{3,2,1,0:T(8,128)(2,1)} %second.1), calls=%async_computation | async-start | bytes 15728640 | tf_op jit(solution)/shard_map/all_to_all | solution.py:401
  225.4 152.1 %copy-start.1 = (s32[1024,15]{0,1:T(8,128)S(1)}, s32[1024,15]{0,1:T(8,128)}, u32[]{:S(2)}) copy-start(s32[1024,15]{0,1:T(8,128)} %param.10) | copy-start | bytes 184324

commit v2 on v0

v2 whole, which is shorter than its diff:
```python
import functools

import jax
import jax.numpy as jnp
from jax import lax
from jax.experimental import pallas as pl
from jax.experimental.pallas import tpu as pltpu
from jax.sharding import PartitionSpec as P

T = 128
R = 8
K = 15
C = 24
TRI = R * (R + 1) // 2
PACK = R * R + TRI - R
VMEM_LIMIT = 63 * 1024 * 1024
BF = jnp.bfloat16
ANY = pl.BlockSpec(memory_space=pl.ANY)
SMEM = pl.BlockSpec(memory_space=pltpu.SMEM)


def up_pieces():
    pieces, off = [], 0
    for col in range(8, 16):
        pieces.append((col, 0, 8, off))
        off += 8
    for u in range(7):
        pieces.append((16 + u, u + 1, 7 - u, off))
        off += 7 - u
    return pieces


def down_pieces():
    pieces, off = [], 0
    for u in range(8):
        pieces.append((u, 0, u + 1, off))
        off += u + 1
    for col in range(8, 15):
        pieces.append((col, 0, 8, off))
        off += 8
    return pieces


def first_pieces():
    pieces, off = [], 0
    for u in range(8):
        pieces.append((16 + u, 0, u + 1, off))
        off += u + 1
    return pieces


def last_pieces():
    pieces, off = [], 0
    for u in range(7):
        pieces.append((u, u + 1, 7 - u, off))
        off += 7 - u
    return pieces


def second_pieces():
    return [(15, 0, 8, 0)]


MESH = pl.DeviceIdType.MESH
OFFSETS = (
    (0, 1), (0, 3), (1, 0), (3, 0), (1, 1), (3, 3), (1, 3), (3, 1),
    (0, 2), (2, 0), (1, 2), (3, 2), (2, 1), (2, 3), (2, 2),
)


def zero_window(win):
    def corner(q, carry):
        win[16 + q, pl.ds(0, 8)] = jnp.zeros((8, T, T), BF)
        win[q, pl.ds(16, 8)] = jnp.zeros((8, T, T), BF)
        return carry

    lax.fori_loop(0, 8, corner, 0)
    for u in range(8):
        win[8 + u, pl.ds(0, u + 1)] = jnp.zeros((u + 1, T, T), BF)
        if u < 7:
            win[8 + u, pl.ds(17 + u, 7 - u)] = jnp.zeros((7 - u, T, T), BF)
    win[23, pl.ds(16, 8)] = jnp.zeros((8, T, T), BF)


def zero_side(win, first_col, row):
    def one(q, carry):
        win[first_col + q, pl.ds(row, 8)] = jnp.zeros((8, T, T), BF)
        return carry

    lax.fori_loop(0, 16, one, 0)


def pack(table, which, raw, dst, base):
    def one(col, carry):
        for t in range(R):
            slot = table[which, col, t]
            tile = raw[jnp.maximum(slot, 0), t]
            dst[col, base + t] = jnp.where(slot >= 0, tile, jnp.zeros_like(tile))
        return carry

    lax.fori_loop(0, C, one, 0)


def band_step(left, win, pair, rows, start, depth, put):
    lhs = jnp.concatenate(
        [left[start + q, pl.ds(2 * rows, 2)].reshape(2 * T, T) for q in range(depth)], axis=1
    )
    rhs = jnp.concatenate(
        [win[2 * pair + h, pl.ds(start, depth)].reshape(depth * T, T) for h in range(2)], axis=1
    )
    total = jnp.dot(lhs, rhs, preferred_element_type=jnp.float32)
    for h in range(2):
        for m in range(2):
            put(2 * pair + h, 2 * rows + m, total[m * T : (m + 1) * T, h * T : (h + 1) * T])


def fused_kernel(
    last, width, table, rcol, srow, z, f, outgoing,
    win, pwin, left, turned, orth, sem_z, sem_f, sem_o,
    zus, zur, zds, zdr, pus, pur, pds, pdr, ezs, ezr, eps, epr,
):
    device = lax.axis_index("row") * width + lax.axis_index("col")
    has_low = device > 0
    has_high = device < last
    wide = (device < 2) | (device > last - 2)
    is_first = device == 0
    is_last = device == last

    loads = [
        pltpu.make_async_copy(z.at[t], orth.at[pl.ds(0, K), t], sem_z.at[t]) for t in range(R)
    ]
    floads = [
        pltpu.make_async_copy(f.at[t], turned.at[pl.ds(0, K), t], sem_f.at[t]) for t in range(R)
    ]
    for copy in loads + floads:
        copy.start()

    def place(dev):
        return (dev // width, lax.rem(dev, width))

    barrier = pltpu.get_barrier_semaphore()

    zero_window(win)
    zero_window(pwin)

    def clear(q, carry):
        pwin[q, pl.ds(8, 8)] = jnp.zeros((8, T, T), BF)
        pwin[16 + q, pl.ds(8, 8)] = jnp.zeros((8, T, T), BF)
        return carry

    lax.fori_loop(0, 8, clear, 0)
    orth[C] = jnp.zeros((R, T, T), BF)

    @pl.when(is_first)
    def _():
        zero_side(win, 0, 0)
        zero_side(pwin, 0, 0)

    @pl.when(is_last)
    def _():
        zero_side(win, 8, 16)
        zero_side(pwin, 8, 16)

    @pl.when(has_low)
    def _():
        pl.semaphore_signal(barrier, inc=1, device_id=place(device - 1), device_id_type=MESH)

    @pl.when(has_high)
    def _():
        pl.semaphore_signal(barrier, inc=1, device_id=place(device + 1), device_id_type=MESH)

    def send(buf, col, row, rows, to_col, to_row, ssem, rsem, dev):
        return pltpu.make_async_remote_copy(
            src_ref=buf.at[col, pl.ds(8 + row, rows)],
            dst_ref=buf.at[to_col, pl.ds(to_row, rows)],
            send_sem=ssem,
            recv_sem=rsem,
            device_id=place(dev),
            device_id_type=MESH,
        )

    def up(buf, which, ss, rs):
        col, row, rows, off = up_pieces()[which]
        return send(buf, col, row, rows, col - 8, row, ss.at[which], rs.at[which], device + 1)

    def down(buf, which, ss, rs):
        col, row, rows, off = down_pieces()[which]
        return send(buf, col, row, rows, col + 8, 16 + row, ss.at[which], rs.at[which], device - 1)

    def up_col(buf, col, ss, rs):
        return send(buf, col, 0, 8, col - 8, 0, ss.at[col - 8], rs.at[col - 8], device + 1)

    def down_col(buf, col, ss, rs):
        return send(buf, col, 0, 8, col + 8, 16, ss.at[col], rs.at[col], device - 1)

    def edge_first(buf, ss, rs):
        return [
            send(buf, col, row, rows, col - 8, row, ss.at[q], rs.at[q], device + 1)
            for q, (col, row, rows, off) in enumerate(first_pieces())
        ]

    def edge_last(buf, ss, rs):
        return [
            send(buf, col, row, rows, col + 8, 16 + row, ss.at[q], rs.at[q], device - 1)
            for q, (col, row, rows, off) in enumerate(last_pieces())
        ]

    def edge_second(buf, ss, rs):
        return [send(buf, 15, 0, 8, 23, 16, ss.at[0], rs.at[0], device - 1)]

    def start_all(copies):
        for copy in copies:
            copy.start()

    for copy in loads:
        copy.wait()
    pack(table, 0, orth, win, 8)

    @pl.when(has_low & has_high)
    def _():
        pl.semaphore_wait(barrier, 2)

    @pl.when(jnp.logical_not(has_low & has_high))
    def _():
        pl.semaphore_wait(barrier, 1)

    @pl.when(has_high)
    def _():
        start_all([up(win, q, zus, zur) for q in range(8)])

    @pl.when(has_low)
    def _():
        start_all([down(win, q, zds, zdr) for q in range(14, 7, -1)])

    @pl.when(device == 1)
    def _():
        start_all(edge_second(win, ezs, ezr))

    @pl.when(has_high)
    def _():
        start_all([up(win, q, zus, zur) for q in range(8, 15)])

    @pl.when(has_low)
    def _():
        start_all([down(win, q, zds, zdr) for q in range(7, -1, -1)])

    @pl.when(is_first)
    def _():
        start_all(edge_first(win, ezs, ezr))

    @pl.when(is_last)
    def _():
        start_all(edge_last(win, ezs, ezr))

    for copy in floads:
        copy.wait()
    pack(table, 1, turned, left, 0)

    def outer(lhs, buf, us, ur, ds, dr, es, er, put):
        def one(q, carry):
            pair = jnp.where(lax.rem(q, 2) == 0, q // 2, 11 - q // 2)

            @pl.when((pair < 4) & has_low)
            def _():
                up_col(buf, 2 * pair + 8, us, ur).wait_recv()
                up_col(buf, 2 * pair + 9, us, ur).wait_recv()

            @pl.when((pair >= 8) & has_high)
            def _():
                down_col(buf, 2 * pair - 8, ds, dr).wait_recv()

            @pl.when((pair >= 8) & (pair < 11) & has_high)
            def _():
                down_col(buf, 2 * pair - 7, ds, dr).wait_recv()

            @pl.when((pair == 11) & is_first)
            def _():
                edge_second(buf, es, er)[0].wait_recv()

            low = jnp.where(pair < 4, 0, pair - 8)
            low = jnp.where(is_first, jnp.where(pair < 4, 4, 0), low)
            low = jnp.where(is_last, jnp.where(pair < 4, 0, 4), low)
            high = jnp.where(is_first | is_last, 4, jnp.minimum(pair, 3) + 1)
            start = jnp.where(pair < 4, 0, 6)

            def rows_step(rows, inner):
                band_step(lhs, buf, pair, rows, start, 18, put)
                return inner

            return lax.fori_loop(low, high, rows_step, carry)

        lax.fori_loop(0, 8, one, 0)

    def wait_middle(buf, us, ur, ds, dr, es, er):
        @pl.when(has_low)
        def _():
            for q in range(8, 15):
                up(buf, q, us, ur).wait_recv()

        @pl.when(has_high)
        def _():
            for q in range(7, -1, -1):
                down(buf, q, ds, dr).wait_recv()

        @pl.when(device == 1)
        def _():
            for copy in edge_first(buf, es, er):
                copy.wait_recv()

        @pl.when(device == last - 1)
        def _():
            for copy in edge_last(buf, es, er):
                copy.wait_recv()

    def middle(lhs, buf, put, after):
        def one(pair, carry):
            @pl.when(jnp.logical_not(wide))
            def _():
                def rows_step(rows, inner):
                    band_step(lhs, buf, pair, rows, 2 * pair - 8, 18, put)
                    return inner

                lax.fori_loop(0, 4, rows_step, 0)

            @pl.when(wide)
            def _():
                def rows_step(rows, inner):
                    band_step(lhs, buf, pair, rows, 0, C, put)
                    return inner

                lax.fori_loop(0, 4, rows_step, 0)

            after(pair)
            return carry

        lax.fori_loop(4, 8, one, 0)

    def put_product(col, row, value):
        pwin[col, 8 + row] = jnp.where(table[2, col, row] > 0, value, 0.0).astype(BF)

    outer(left, win, zus, zur, zds, zdr, ezs, ezr, put_product)
    @pl.when(has_high)
    def _():
        start_all([up(pwin, q, pus, pur) for q in range(8, 15)])

    @pl.when(has_low)
    def _():
        start_all([down(pwin, q, pds, pdr) for q in range(7, -1, -1)])

    @pl.when(is_first)
    def _():
        start_all(edge_first(pwin, eps, epr))

    @pl.when(is_last)
    def _():
        start_all(edge_last(pwin, eps, epr))

    wait_middle(win, zus, zur, zds, zdr, ezs, ezr)

    def send_pair(pair):
        @pl.when(has_high)
        def _():
            start_all([up_col(pwin, 2 * pair + h, pus, pur) for h in range(2)])

        @pl.when(has_low)
        def _():
            down_col(pwin, 2 * pair, pds, pdr).start()

        @pl.when(has_low & (pair < 7))
        def _():
            down_col(pwin, 2 * pair + 1, pds, pdr).start()

        @pl.when((pair == 7) & (device == 1))
        def _():
            start_all(edge_second(pwin, eps, epr))

    def send_before(pair):
        @pl.when(pair > 4)
        def _():
            send_pair(pair - 1)

    middle(left, win, put_product, send_before)

    def turn(k, carry):
        for a in range(R):
            turned[k, a] = win[8 + a, k].T
        return carry

    lax.fori_loop(0, 2, turn, 0)
    send_pair(jnp.int32(7))
    lax.fori_loop(2, C, turn, 0)

    def put_orth(col, row, value):
        orth[col, row] = value.astype(BF)

    wait_middle(pwin, pus, pur, pds, pdr, eps, epr)
    middle(turned, pwin, put_orth, lambda pair: None)
    outer(turned, pwin, pus, pur, pds, pdr, eps, epr, put_orth)

    def wait_sends(buf, us, ur, ds, dr, es, er):
        @pl.when(has_high)
        def _():
            for q in range(15):
                up(buf, q, us, ur).wait_send()

        @pl.when(has_low)
        def _():
            for q in range(15):
                down(buf, q, ds, dr).wait_send()

        for which, copies in ((0, edge_first), (1, edge_second), (last, edge_last)):

            @pl.when(device == which)
            def _():
                for copy in copies(buf, es, er):
                    copy.wait_send()

    wait_sends(win, zus, zur, zds, zdr, ezs, ezr)

    def deliver(e, carry):
        row = srow[e]
        for s in range(K):
            win[e, s] = orth[rcol[row, s], row]
        return carry

    lax.fori_loop(0, width, deliver, 0)
    outs = [
        pltpu.make_async_copy(win.at[e, pl.ds(0, K)], outgoing.at[e], sem_o.at[e])
        for e in range(width)
    ]
    start_all(outs)
    wait_sends(pwin, pus, pur, pds, pdr, eps, epr)
    for copy in outs:
        copy.wait()


def exchange_kernel(width, side, source, target, bounce, ssem, rsem, lsem):
    row = lax.axis_index("row")
    col = lax.axis_index("col")
    def at(o):
        return lax.rem(col // side + o[0], side) * side + lax.rem(col + o[1], side)

    barrier = pltpu.get_barrier_semaphore()
    for o in OFFSETS:
        pl.semaphore_signal(barrier, inc=1, device_id=(row, at(o)), device_id_type=MESH)
    pl.semaphore_wait(barrier, width - 1)
    copies = []
    for q, o in enumerate(OFFSETS):
        copy = pltpu.make_async_remote_copy(
            src_ref=source.at[at(o)],
            dst_ref=target.at[col],
            send_sem=ssem.at[q],
            recv_sem=rsem.at[q],
            device_id=(row, at(o)),
            device_id_type=MESH,
        )
        copy.start()
        copies.append(copy)
    mine = pltpu.make_async_copy(source.at[col], bounce, lsem.at[0])
    mine.start()
    mine.wait()
    back = pltpu.make_async_copy(bounce, target.at[col], lsem.at[1])
    back.start()
    back.wait()
    for copy in copies:
        copy.wait()


def take_kernel(source, incoming, out):
    out[...] = incoming[...]


def body(
    fock_tiles, fock_pattern, basis_tiles, basis_pattern, product_pattern, result_pattern, new_index
):
    total_rows = fock_pattern.shape[0]
    width = lax.axis_size("col")
    last = lax.axis_size("row") * width - 1
    device = lax.axis_index(("row", "col"))
    first_row = device * R

    def relative(pattern):
        own = lax.dynamic_slice_in_dim(pattern, first_row, R, 0)
        return jnp.where(own >= 0, own - first_row + 8, C)

    patterns = jnp.stack(
        [relative(basis_pattern), relative(fock_pattern), relative(product_pattern)]
    )
    cols = jnp.arange(C, dtype=jnp.int32)[None, :, None, None]
    slots = jnp.arange(1, K + 1, dtype=jnp.int32)
    table = jnp.sum(jnp.where(patterns[:, None] == cols, slots, 0), axis=-1) - 1
    table = jnp.where(jnp.arange(3)[:, None, None] < 2, table, (table >= 0).astype(jnp.int32))
    rcol = relative(result_pattern)
    own_new = lax.dynamic_slice_in_dim(new_index, first_row, R, 0)
    dest = own_new // R % width
    srow = jnp.sum(
        jnp.where(
            dest[None, :] == jnp.arange(width, dtype=jnp.int32)[:, None],
            jnp.arange(R, dtype=jnp.int32)[None, :],
            0,
        ),
        axis=1,
    )
    dma = pltpu.SemaphoreType.DMA
    outgoing = pl.pallas_call(
        functools.partial(fused_kernel, last, width),
        out_shape=jax.ShapeDtypeStruct((width, K, T, T), BF),
        in_specs=[SMEM] * 3 + [ANY] * 2,
        out_specs=ANY,
        scratch_shapes=[
            pltpu.VMEM((C, C, T, T), BF),
            pltpu.VMEM((C, C, T, T), BF),
            pltpu.VMEM((C, R, T, T), BF),
            pltpu.VMEM((C, R, T, T), BF),
            pltpu.VMEM((C + 1, R, T, T), BF),
            dma((R,)),
            dma((R,)),
            dma((width,)),
        ]
        + [dma((15,))] * 8
        + [dma((8,))] * 4,
        compiler_params=pltpu.CompilerParams(
            vmem_limit_bytes=VMEM_LIMIT, collective_id=0, has_side_effects=True
        ),
        name="fused",
    )(table, rcol, srow, basis_tiles, fock_tiles)
    incoming = pl.pallas_call(
        functools.partial(exchange_kernel, width, 4),
        out_shape=jax.ShapeDtypeStruct((width, K, T, T), BF),
        in_specs=[ANY],
        out_specs=ANY,
        scratch_shapes=[
            pltpu.VMEM((K, T, T), BF),
            dma((width - 1,)),
            dma((width - 1,)),
            dma((2,)),
        ],
        compiler_params=pltpu.CompilerParams(collective_id=1, has_side_effects=True),
        name="exchange",
    )(outgoing)
    wanted = first_row + jnp.arange(R, dtype=jnp.int32)
    found = new_index[None, :] == wanted[:, None]
    anchor = jnp.sum(
        jnp.where(found, jnp.arange(total_rows, dtype=jnp.int32)[None, :], 0), axis=1
    )
    source = anchor // R % width
    return pl.pallas_call(
        take_kernel,
        grid_spec=pltpu.PrefetchScalarGridSpec(
            num_scalar_prefetch=1,
            grid=(R,),
            in_specs=[pl.BlockSpec((1, K, T, T), lambda q, s: (s[q], 0, 0, 0))],
            out_specs=pl.BlockSpec((1, K, T, T), lambda q, s: (q, 0, 0, 0)),
        ),
        out_shape=jax.ShapeDtypeStruct((R, K, T, T), BF),
        name="take",
    )(source, incoming)


def solution(mesh):
    placed = (
        P(("row", "col"), None, None, None),
        P(),
        P(("row", "col"), None, None, None),
        P(),
        P(),
        P(),
        P(),
    )
    return jax.shard_map(
        body,
        mesh=mesh,
        in_specs=placed,
        out_specs=P(("row", "col"), None, None, None),
        check_vma=False,
    )
```

time: 1080 us -> 275 us (0.25); the launches traced: 1070 us -> 273 us
  waiting for transfers between devices: 310 us -> 0 us
  other arithmetic: 293 us -> 4.23 us
  Pallas kernels: 0 us -> 266 us
  local copies, waits for them, and re-layouts: 243 us -> 2.13 us
  matrix products: 198 us -> 0 us
  starting transfers between devices: 21.8 us -> 0 us
    pallas_call x0 -> x3, Pallas kernels: none -> 266 us  [the longest x1 153 us: body(): pl.pallas_call(functools.partial(fused_kernel, last, width), out_shape=ja...]
    scatter-add x8 -> x0, other arithmetic: 259 us -> none  [push_row(): return partial_value.at[offsets].add(terms)]
    dot_general x32 -> x0, matrix products: 198 us -> none  [the longest x8 75.8 us: push_row(): jnp.einsum('sba,srbc->srac', row_tiles, picked, preferred_element_type=jn...]
    ppermute x4 -> x0, waiting for transfers between devices: 170 us -> none  [the longest x2 87.1 us: passed_along(): return lax.ppermute(array, axis, pairs)]
    all_to_all x1 -> x0, waiting for transfers between devices: 140 us -> none  [body(): lax.all_to_all(outgoing, 'col', split_axis=0, concat_axis=0, tiled=True)]
    mul x8 -> x0, local copies, waits for them, and re-layouts: 123 us -> none  [push_row(): terms = terms * valid.astype(jnp.float32)[:, None, None, None]]
    gather x26 -> x0, local copies, waits for them, and re-layouts: 92.7 us -> none  [the longest x8 70.8 us: first_product(): gathered = basis_near[near_index]]
    ppermute x4 -> x0, starting transfers between devices: 17.1 us -> none  [the longest x2 7.28 us: passed_along(): return lax.ppermute(array, axis, pairs)]
  transfers between devices with their start and end apart: 5 -> 0, of which waited for: 5 -> 0; matrix products, arithmetic and copies ran while one was open for 0% -> 0% of each run, Pallas kernels for 0% -> 0%
where the time goes in v2:
time: 275 us; the launch traced here: 273 us
  Pallas kernels  266 us (97%)
  other arithmetic  4.23 us (2%)
    pallas_call x1, Pallas kernels, body(): pl.pallas_call(functools.partial(fused_kernel, last, width), out_shape=ja...  153 us
    pallas_call x1, Pallas kernels, body(): pl.pallas_call(functools.partial(exchange_kernel, width, 4), out_shape=ja...  106 us
    pallas_call x1, Pallas kernels, body(): pl.pallas_call(take_kernel, grid_spec=pltpu.PrefetchScalarGridSpec(num_sc...  7.15 us

profile of v2, /device:TPU:8, one launch (start us, length us, event | category | flops | bytes accessed | tf_op | source)
XLA Modules:
  0.0 272.6 jit_solution(9159768801098755607)
XLA Ops:
  0.0 0.0 copy-start
  0.0 0.9 select_reduce_fusion.1
  0.9 1.2 and_select_fusion
  2.2 0.6 select_reduce_fusion.2.srow
  2.8 0.0 copy-done
  2.8 0.1 constant_dynamic-slice_fusion.2
  2.9 0.1 copy.19
  3.0 0.8 constant_dynamic-slice_fusion.1
  3.7 0.1 copy.20
  3.8 0.8 constant_dynamic-slice_fusion
  4.6 0.1 copy.21
  4.7 0.6 add_select_fusion.rcol
  5.3 0.1 copy.18
  5.4 0.1 copy.15
  5.5 0.1 select_reduce_fusion
  5.6 0.1 copy.16
  5.7 0.7 convert_select_fusion.table
  6.4 152.8 %fused.1.source = bf16[16,15,128,128]{3,2,1,0:T(8,128)(2,1)} custom-call(s32[3,24,8]{2,1,0:T(8,128)} %convert_select_fusion.table, s32[8,15]{1,0:T(8,128)} %add_select_fusion.rcol, s32[16]{0:T(128)} %select_reduce_fusion.2.srow, bf16[8,15,128,128]{3,2,1,0:T(8,128)(2,1)} %z.1, bf16[8,15,128,128]{3,2,1,0:T(8,128)(2,1)} %f.1), custom_call_target="tpu_custom_call" | custom-call | tf_op jit(solution)/shard_map/fused/pallas_call | solution.py:505
  159.2 106.2 %exchange.1.incoming = bf16[16,15,128,128]{3,2,1,0:T(8,128)(2,1)} custom-call(bf16[16,15,128,128]{3,2,1,0:T(8,128)(2,1)} %fused.1.source), custom_call_target="tpu_custom_call" | custom-call | tf_op jit(solution)/shard_map/exchange/pallas_call | solution.py:527
  265.4 7.2 %take.1 = bf16[8,15,128,128]{3,2,1,0:T(8,128)(2,1)} custom-call(s32[8]{0:T(128)} %get-tuple-element.8.source, bf16[16,15,128,128]{3,2,1,0:T(8,128)(2,1)} %exchange.1.incoming), custom_call_target="tpu_custom_call" | custom-call | tf_op jit(solution)/shard_map/take/pallas_call | solution.py:547
  (6 shorter events, 0.0 us)
Async XLA Ops:
  0.0 2.8 %copy-start = (s32[1024,15]{0,1:T(8,128)S(1)}, s32[1024,15]{0,1:T(8,128)}, u32[]{:S(2)}) copy-start(s32[1024,15]{0,1:T(8,128)} %param.8) | copy-start | bytes 184324

commit v3 on v2

v3 whole, which is shorter than its diff:
```python
import functools

import jax
import jax.numpy as jnp
from jax import lax
from jax.experimental import pallas as pl
from jax.experimental.pallas import tpu as pltpu
from jax.sharding import PartitionSpec as P

T = 128
R = 8
K = 15
C = 24
VMEM_LIMIT = 63 * 1024 * 1024
BF = jnp.bfloat16
ANY = pl.BlockSpec(memory_space=pl.ANY)
SMEM = pl.BlockSpec(memory_space=pltpu.SMEM)


MESH = pl.DeviceIdType.MESH
OFFSETS = (
    (0, 1), (0, 3), (1, 0), (3, 0), (1, 1), (3, 3), (1, 3), (3, 1),
    (0, 2), (2, 0), (1, 2), (3, 2), (2, 1), (2, 3), (2, 2),
)


def zero_window(win, first_col, row):
    def corner(q, carry):
        win[16 + q, pl.ds(0, 8)] = jnp.zeros((8, T, T), BF)
        win[q, pl.ds(16, 8)] = jnp.zeros((8, T, T), BF)
        return carry

    lax.fori_loop(0, 8, corner, 0)
    for u in range(8):
        win[8 + u, pl.ds(0, u + 1)] = jnp.zeros((u + 1, T, T), BF)
        if u < 7:
            win[8 + u, pl.ds(17 + u, 7 - u)] = jnp.zeros((7 - u, T, T), BF)
    win[23, pl.ds(16, 8)] = jnp.zeros((8, T, T), BF)
    for q in range(8):
        win[first_col + q, row] = jnp.zeros((T, T), BF)


def zero_side(win, first_col, row):
    def one(q, carry):
        win[first_col + q, pl.ds(row, 8)] = jnp.zeros((8, T, T), BF)
        return carry

    lax.fori_loop(0, 16, one, 0)


def pack(table, which, raw, dst, base):
    def one(col, carry):
        for t in range(R):
            slot = table[which, col, t]
            tile = raw[jnp.maximum(slot, 0), t]
            dst[col, base + t] = jnp.where(slot >= 0, tile, jnp.zeros_like(tile))
        return carry

    lax.fori_loop(0, C, one, 0)


def band_step(left, win, pair, rows, start, depth, put):
    lhs = jnp.concatenate(
        [left[start + q, pl.ds(2 * rows, 2)].reshape(2 * T, T) for q in range(depth)], axis=1
    )
    rhs = jnp.concatenate(
        [win[2 * pair + h, pl.ds(start, depth)].reshape(depth * T, T) for h in range(2)], axis=1
    )
    total = jnp.dot(lhs, rhs, preferred_element_type=jnp.float32)
    for h in range(2):
        for m in range(2):
            put(2 * pair + h, 2 * rows + m, total[m * T : (m + 1) * T, h * T : (h + 1) * T])


def fused_kernel(
    last, width, side, table, rel, new_index, z, f, incoming,
    win, pwin, left, turned, orth, sem_z, sem_f, sem_o,
    zus, zur, zds, zdr, pus, pur, pds, pdr, ezs, ezr, eps, epr, xs, xr,
):
    mesh_row = lax.axis_index("row")
    mesh_col = lax.axis_index("col")
    device = mesh_row * width + mesh_col
    has_low = device > 0
    has_high = device < last
    wide = (device < 2) | (device > last - 2)
    is_first = device == 0
    is_last = device == last

    loads = [
        pltpu.make_async_copy(z.at[t], orth.at[pl.ds(0, K), t], sem_z.at[t]) for t in range(R)
    ]
    floads = [
        pltpu.make_async_copy(f.at[t], turned.at[pl.ds(0, K), t], sem_f.at[t]) for t in range(R)
    ]
    for copy in loads + floads:
        copy.start()

    def place(dev):
        return (dev // width, lax.rem(dev, width))

    def peer(o):
        col = lax.rem(mesh_col // side + o[0], side) * side + lax.rem(mesh_col + o[1], side)
        return col

    barrier = pltpu.get_barrier_semaphore()
    for o in OFFSETS:
        pl.semaphore_signal(barrier, inc=1, device_id=(mesh_row, peer(o)), device_id_type=MESH)

    zero_window(win, 16, 23)

    @pl.when(is_first)
    def _():
        zero_side(win, 0, 0)

    @pl.when(is_last)
    def _():
        zero_side(win, 8, 16)

    @pl.when(has_low)
    def _():
        pl.semaphore_signal(barrier, inc=1, device_id=place(device - 1), device_id_type=MESH)

    @pl.when(has_high)
    def _():
        pl.semaphore_signal(barrier, inc=1, device_id=place(device + 1), device_id_type=MESH)

    def send(buf, col, row, rows, to_col, to_row, ssem, rsem, dev):
        return pltpu.make_async_remote_copy(
            src_ref=buf.at[col, pl.ds(8 + row, rows)],
            dst_ref=buf.at[to_col, pl.ds(to_row, rows)],
            send_sem=ssem,
            recv_sem=rsem,
            device_id=place(dev),
            device_id_type=MESH,
        )

    def up_col(buf, col, ss, rs, skip):
        return send(
            buf, col, skip, 8 - skip, col - 8, skip, ss.at[col - 8], rs.at[col - 8], device + 1
        )

    def down_col(buf, col, ss, rs, skip):
        return send(buf, col, 0, 8 - skip, col + 8, 16, ss.at[col], rs.at[col], device - 1)

    def up_tri(buf, ss, rs):
        return [
            send(buf, 16 + u, u + 1, 7 - u, 8 + u, u + 1, ss.at[8 + u], rs.at[8 + u], device + 1)
            for u in range(7)
        ]

    def down_tri(buf, ss, rs):
        return [
            send(buf, u, 0, u + 1, 8 + u, 16, ss.at[u], rs.at[u], device - 1)
            for u in range(7, -1, -1)
        ]

    def apart(buf, first_col, cols, row, to_col, to_row, ssem, rsem, dev):
        return pltpu.make_async_remote_copy(
            src_ref=buf.at[pl.ds(first_col, cols), row],
            dst_ref=buf.at[pl.ds(to_col, cols), to_row],
            send_sem=ssem,
            recv_sem=rsem,
            device_id=place(dev),
            device_id_type=MESH,
        )

    def edge_first(buf, ss, rs):
        return [
            send(buf, 16 + u, 0, u + 1, 8 + u, 0, ss.at[u], rs.at[u], device + 1)
            for u in range(8)
        ]

    def edge_first_row(buf, ss, rs):
        return [apart(buf, 8, 8, 8, 0, 0, ss.at[8], rs.at[8], device + 1)]

    def edge_last(buf, ss, rs):
        return [
            send(buf, u, u + 1, 7 - u, 8 + u, 17 + u, ss.at[u], rs.at[u], device - 1)
            for u in range(7)
        ]

    def edge_second(buf, ss, rs):
        return [send(buf, 15, 0, 8, 23, 16, ss.at[0], rs.at[0], device - 1)]

    def edge_second_row(buf, ss, rs):
        return [apart(buf, 8, 7, 15, 16, 23, ss.at[8], rs.at[8], device - 1)]

    def start_all(copies):
        for copy in copies:
            copy.start()

    for copy in loads:
        copy.wait()
    pack(table, 0, orth, win, 8)

    @pl.when(has_low & has_high)
    def _():
        pl.semaphore_wait(barrier, width + 1)

    @pl.when(jnp.logical_not(has_low & has_high))
    def _():
        pl.semaphore_wait(barrier, width)

    @pl.when(has_high)
    def _():
        start_all([up_col(win, col, zus, zur, 0) for col in range(8, 16)])

    @pl.when(has_low)
    def _():
        start_all([down_col(win, col, zds, zdr, 1) for col in range(14, 7, -1)])

    @pl.when(device == 1)
    def _():
        start_all(edge_second(win, ezs, ezr) + edge_second_row(win, ezs, ezr))

    zero_window(pwin, 0, 0)

    def clear(q, carry):
        pwin[q, pl.ds(8, 8)] = jnp.zeros((8, T, T), BF)
        pwin[16 + q, pl.ds(8, 8)] = jnp.zeros((8, T, T), BF)
        return carry

    lax.fori_loop(0, 8, clear, 0)
    orth[C] = jnp.zeros((R, T, T), BF)

    @pl.when(is_first)
    def _():
        zero_side(pwin, 0, 0)

    @pl.when(is_last)
    def _():
        zero_side(pwin, 8, 16)

    @pl.when(has_high)
    def _():
        start_all(up_tri(win, zus, zur))

    @pl.when(has_low)
    def _():
        start_all(down_tri(win, zds, zdr))

    @pl.when(is_first)
    def _():
        start_all(edge_first(win, ezs, ezr))

    @pl.when(is_last)
    def _():
        start_all(edge_last(win, ezs, ezr))

    for copy in floads:
        copy.wait()
    pack(table, 1, turned, left, 0)

    def outer(lhs, buf, us, ur, ds, dr, es, er, put, second):
        skip_up, skip_down = (1, 0) if second else (0, 1)

        def one(q, carry):
            half = q // 2
            if second:
                pair = jnp.where(lax.rem(q, 2) == 0, 3 - half, 8 + half)
            else:
                pair = jnp.where(lax.rem(q, 2) == 0, half, 11 - half)

            @pl.when((pair < 4) & has_low)
            def _():
                up_col(buf, 2 * pair + 8, us, ur, skip_up).wait_recv()
                up_col(buf, 2 * pair + 9, us, ur, skip_up).wait_recv()

            @pl.when((pair >= 8) & has_high)
            def _():
                down_col(buf, 2 * pair - 8, ds, dr, skip_down).wait_recv()

            @pl.when((pair >= 8) & (pair < 11) & has_high)
            def _():
                down_col(buf, 2 * pair - 7, ds, dr, skip_down).wait_recv()

            if second:

                @pl.when((q == 0) & (device == 1))
                def _():
                    edge_first_row(buf, es, er)[0].wait_recv()

                @pl.when((pair == 11) & is_first)
                def _():
                    edge_second(buf, es, er)[0].wait_recv()
            else:

                @pl.when((pair == 11) & is_first)
                def _():
                    edge_second(buf, es, er)[0].wait_recv()
                    edge_second_row(buf, es, er)[0].wait_recv()

            low = jnp.where(pair < 4, 0, pair - 8)
            low = jnp.where(is_first, jnp.where(pair < 4, 4, 0), low)
            low = jnp.where(is_last, jnp.where(pair < 4, 0, 4), low)
            high = jnp.where(is_first | is_last, 4, jnp.minimum(pair, 3) + 1)
            start = jnp.where(pair < 4, 0, 6)

            def rows_step(rows, inner):
                band_step(lhs, buf, pair, rows, start, 18, put)
                return inner

            return lax.fori_loop(low, high, rows_step, carry)

        lax.fori_loop(0, 8, one, 0)

    def wait_middle(buf, us, ur, ds, dr, es, er):
        @pl.when(has_low)
        def _():
            for copy in up_tri(buf, us, ur):
                copy.wait_recv()

        @pl.when(has_high)
        def _():
            for copy in down_tri(buf, ds, dr):
                copy.wait_recv()

        @pl.when(device == 1)
        def _():
            for copy in edge_first(buf, es, er):
                copy.wait_recv()

        @pl.when(device == last - 1)
        def _():
            for copy in edge_last(buf, es, er):
                copy.wait_recv()

    def middle(lhs, buf, put, after):
        def one(q, carry):
            pair = jnp.where(lax.rem(q, 2) == 0, 7 - q // 2, 4 + q // 2)

            @pl.when(jnp.logical_not(wide))
            def _():
                def rows_step(rows, inner):
                    band_step(lhs, buf, pair, rows, 2 * pair - 8, 18, put)
                    return inner

                lax.fori_loop(0, 4, rows_step, 0)

            @pl.when(wide)
            def _():
                def rows_step(rows, inner):
                    band_step(lhs, buf, pair, rows, 0, C, put)
                    return inner

                lax.fori_loop(0, 4, rows_step, 0)

            after(q)
            return carry

        lax.fori_loop(0, 4, one, 0)

    def put_product(col, row, value):
        pwin[col, 8 + row] = jnp.where(table[2, col, row] >= 0, value, 0.0).astype(BF)

    outer(left, win, zus, zur, zds, zdr, ezs, ezr, put_product, False)

    @pl.when(has_high)
    def _():
        start_all(up_tri(pwin, pus, pur))

    @pl.when(has_low)
    def _():
        start_all(down_tri(pwin, pds, pdr))

    wait_middle(win, zus, zur, zds, zdr, ezs, ezr)

    @pl.when(is_first)
    def _():
        start_all(edge_first(pwin, eps, epr))

    @pl.when(is_last)
    def _():
        start_all(edge_last(pwin, eps, epr))

    def send_up(pair):
        @pl.when(has_high)
        def _():
            start_all([up_col(pwin, 2 * pair + h, pus, pur, 1) for h in range(2)])

    def send_down(pair):
        @pl.when(has_low)
        def _():
            down_col(pwin, 2 * pair, pds, pdr, 0).start()

        @pl.when(has_low & (pair < 7))
        def _():
            down_col(pwin, 2 * pair + 1, pds, pdr, 0).start()

    def send_ready(q):
        @pl.when(q == 1)
        def _():
            send_up(7)

            @pl.when(device == 1)
            def _():
                start_all(edge_second(pwin, eps, epr))

        @pl.when(q == 2)
        def _():
            send_down(4)

        @pl.when(q == 3)
        def _():
            send_up(6)

    middle(left, win, put_product, send_ready)

    def turn(k, carry):
        for a in range(R):
            turned[k, a] = win[8 + a, k].T
        return carry

    lax.fori_loop(0, 2, turn, 0)
    send_up(5)
    send_down(5)
    send_up(4)
    send_down(6)
    send_down(7)

    @pl.when(is_first)
    def _():
        start_all(edge_first_row(pwin, eps, epr))

    lax.fori_loop(2, C, turn, 0)

    def put_orth(col, row, value):
        orth[col, row] = value.astype(BF)

    wait_middle(pwin, pus, pur, pds, pdr, eps, epr)
    middle(turned, pwin, put_orth, lambda q: None)
    outer(turned, pwin, pus, pur, pds, pdr, eps, epr, put_orth, True)

    def wait_sends(buf, us, ur, ds, dr, es, er, product):
        def drain(copies):
            for copy in copies:
                copy.wait_send()

        @pl.when(has_high)
        def _():
            drain([up_col(buf, col, us, ur, product) for col in range(8, 16)])
            drain(up_tri(buf, us, ur))

        @pl.when(has_low)
        def _():
            drain([down_col(buf, col, ds, dr, 1 - product) for col in range(8, 15)])
            drain(down_tri(buf, ds, dr))

        @pl.when(is_first)
        def _():
            drain(edge_first(buf, es, er))
            if product:
                drain(edge_first_row(buf, es, er))

        @pl.when(device == 1)
        def _():
            drain(edge_second(buf, es, er))
            if not product:
                drain(edge_second_row(buf, es, er))

        @pl.when(is_last)
        def _():
            drain(edge_last(buf, es, er))

    def stage(e):
        row = jnp.int32(0)
        for t in range(R):
            there = lax.rem(new_index[device * R + t] // R, width)
            row = jnp.where(there == e, t, row)
        for s in range(K):
            win[e, s] = orth[rel[3, row, s], row]

    wait_sends(win, zus, zur, zds, zdr, ezs, ezr, 0)

    packets = []
    for q, o in enumerate(OFFSETS):
        stage(peer(o))
        packets.append(
            pltpu.make_async_remote_copy(
                src_ref=win.at[peer(o), pl.ds(0, K)],
                dst_ref=incoming.at[mesh_col],
                send_sem=xs.at[q],
                recv_sem=xr.at[q],
                device_id=(mesh_row, peer(o)),
                device_id_type=MESH,
            )
        )
        if q:
            packets[q - 1].start()
    stage(mesh_col)
    packets[-1].start()
    mine = pltpu.make_async_copy(win.at[mesh_col, pl.ds(0, K)], incoming.at[mesh_col], sem_o)
    mine.start()
    wait_sends(pwin, pus, pur, pds, pdr, eps, epr, 1)
    mine.wait()
    for packet in packets:
        packet.wait()


def take_kernel(width, new_index, incoming, out, held, sem_in, sem_out):
    device = lax.axis_index("row") * width + lax.axis_index("col")
    group = device // width * width

    def row(q, carry):
        def look(j, found):
            hit = new_index[(group + j) * R + q] == device * R + q
            return jnp.where(hit, j, found)

        source = lax.fori_loop(0, width, look, 0)
        pltpu.make_async_copy(incoming.at[source], held.at[q], sem_in.at[q]).start()
        return carry

    lax.fori_loop(0, R, row, 0)
    outs = []
    for q in range(R):
        pltpu.make_async_copy(incoming.at[0], held.at[q], sem_in.at[q]).wait()
        outs.append(pltpu.make_async_copy(held.at[q], out.at[q], sem_out.at[q]))
        outs[q].start()
    for copy in outs:
        copy.wait()


def body(
    fock_tiles, fock_pattern, basis_tiles, basis_pattern, product_pattern, result_pattern, new_index
):
    width = lax.axis_size("col")
    last = lax.axis_size("row") * width - 1
    device = lax.axis_index(("row", "col"))
    first_row = device * R

    def own(pattern):
        return lax.dynamic_slice_in_dim(pattern, first_row, R, 0)

    rel = jnp.stack(
        [own(basis_pattern), own(fock_pattern), own(product_pattern), own(result_pattern)]
    )
    rel = jnp.where(rel >= 0, rel - first_row + 8, C)
    cols = jnp.arange(C, dtype=jnp.int32)[None, :, None, None]
    slots = jnp.arange(1, K + 1, dtype=jnp.int32)
    table = jnp.sum(jnp.where(rel[:3, None] == cols, slots, 0), axis=-1) - 1
    dma = pltpu.SemaphoreType.DMA
    incoming = pl.pallas_call(
        functools.partial(fused_kernel, last, width, 4),
        out_shape=jax.ShapeDtypeStruct((width, K, T, T), BF),
        in_specs=[SMEM] * 3 + [ANY] * 2,
        out_specs=ANY,
        scratch_shapes=[
            pltpu.VMEM((C, C, T, T), BF),
            pltpu.VMEM((C, C, T, T), BF),
            pltpu.VMEM((C, R, T, T), BF),
            pltpu.VMEM((C, R, T, T), BF),
            pltpu.VMEM((C + 1, R, T, T), BF),
            dma((R,)),
            dma((R,)),
            dma,
        ]
        + [dma((15,))] * 8
        + [dma((9,))] * 4
        + [dma((width - 1,))] * 2,
        compiler_params=pltpu.CompilerParams(
            vmem_limit_bytes=VMEM_LIMIT, collective_id=0, has_side_effects=True
        ),
        name="fused",
    )(table, rel, new_index, basis_tiles, fock_tiles)
    return pl.pallas_call(
        functools.partial(take_kernel, width),
        out_shape=jax.ShapeDtypeStruct((R, K, T, T), BF),
        in_specs=[SMEM, ANY],
        out_specs=ANY,
        scratch_shapes=[pltpu.VMEM((R, K, T, T), BF), dma((R,)), dma((R,))],
        name="take",
    )(new_index, incoming)


def solution(mesh):
    placed = (
        P(("row", "col"), None, None, None),
        P(),
        P(("row", "col"), None, None, None),
        P(),
        P(),
        P(),
        P(),
    )
    return jax.shard_map(
        body,
        mesh=mesh,
        in_specs=placed,
        out_specs=P(("row", "col"), None, None, None),
        check_vma=False,
    )
```

time: 275 us -> 285 us (1.036)
  the two profiles are of different devices: /device:TPU:8 before, /device:TPU:100 now
where the time goes in v3:
time: 285 us
  Pallas kernels  282 us (99%)
    pallas_call x1, Pallas kernels, body(): pl.pallas_call(functools.partial(fused_kernel, last, width, 4), out_shape...  277 us

profile of v3, /device:TPU:100, one launch (start us, length us, event | category | flops | bytes accessed | tf_op | source)
XLA Modules:
  0.0 284.8 jit_solution(18190098828574463047)
XLA Ops:
  0.0 0.8 constant_dynamic-slice_fusion.2
  0.8 0.1 copy.26
  0.9 0.1 copy.25
  1.0 0.8 constant_dynamic-slice_fusion
  1.7 0.1 copy.28
  1.8 0.1 copy.27
  1.9 0.0 copy-start
  1.9 0.1 copy.22
  2.0 0.1 select_reduce_fusion
  2.2 0.1 copy.23
  2.2 0.6 broadcast_add_fusion.table
  2.9 0.0 copy-done
  2.9 277.2 %fused.1.incoming = bf16[16,15,128,128]{3,2,1,0:T(8,128)(2,1)} custom-call(s32[3,24,8]{2,1,0:T(8,128)} %broadcast_add_fusion.table, s32[4,8,15]{2,1,0:T(8,128)} %copy-done, s32[1024]{0:T(1024)} %new_index.3, bf16[8,15,128,128]{3,2,1,0:T(8,128)(2,1)} %z.1, bf16[8,15,128,128]{3,2,1,0:T(8,128)(2,1)} %f.1), custom_call_target="tpu_custom_call" | custom-call | tf_op jit(solution)/shard_map/fused/pallas_call | solution.py:542
  280.1 4.7 %take.1 = bf16[8,15,128,128]{3,2,1,0:T(8,128)(2,1)} custom-call(s32[1024]{0:T(1024)} %new_index.3, bf16[16,15,128,128]{3,2,1,0:T(8,128)(2,1)} %fused.1.incoming), custom_call_target="tpu_custom_call" | custom-call | tf_op jit(solution)/shard_map/take/pallas_call | solution.py:565
  (3 shorter events, 0.0 us)
Async XLA Ops:
  1.9 1.0 copy-start

commit v4 on v3

--- a/solution.py
+++ b/solution.py
@@ -22,6 +22,30 @@
     (0, 1), (0, 3), (1, 0), (3, 0), (1, 1), (3, 3), (1, 3), (3, 1),
     (0, 2), (2, 0), (1, 2), (3, 2), (2, 1), (2, 3), (2, 2),
 )
+
+
+PARTS = 3
+ROUTES = 4
+FIRST = (
+    tuple((("c", 23 - k, 0, 8 - k), ("c", 16 + k, 0, k + 1)) for k in range(ROUTES)),
+    tuple(
+        (("c", 23 - k, 0, 8 - k), ("c", 16 + k, 0, k + 1), ("r", 8 + 2 * k, 0, 2))
+        for k in range(ROUTES)
+    ),
+)
+LAST = (
+    (
+        (("c", 0, 1, 7),),
+        (("c", 1, 2, 6), ("c", 6, 7, 1)),
+        (("c", 2, 3, 5), ("c", 5, 6, 2)),
+        (("c", 3, 4, 4), ("c", 4, 5, 3)),
+    ),
+) * 2
+SECOND = (
+    ((("c", 15, 0, 4),), (("c", 15, 4, 4),), (("r", 8, 7, 4),), (("r", 12, 7, 3),)),
+    tuple((("c", 15, 2 * k, 2),) for k in range(ROUTES)),
+)
+HOLD = 11
 
 
 def zero_window(win, first_col, row):
@@ -75,7 +99,7 @@
 def fused_kernel(
     last, width, side, table, rel, new_index, z, f, incoming,
     win, pwin, left, turned, orth, sem_z, sem_f, sem_o,
-    zus, zur, zds, zdr, pus, pur, pds, pdr, ezs, ezr, eps, epr, xs, xr,
+    zus, zur, zds, zdr, pus, pur, pds, pdr, hold, es, er, hs, hr, xs, xr,
 ):
     mesh_row = lax.axis_index("row")
     mesh_col = lax.axis_index("col")
@@ -102,7 +126,115 @@
         col = lax.rem(mesh_col // side + o[0], side) * side + lax.rem(mesh_col + o[1], side)
         return col
 
+    def relays(receiver):
+        row, col = divmod(receiver, width)
+        rows = (last + 1) // width
+        return [
+            row * width + (col + side) % width,
+            row * width + (col - side) % width,
+            (row + 2) % rows * width + col,
+            (row - 2) % rows * width + col,
+        ]
+
+    flows = [(0, 1, True, FIRST), (last, last - 1, False, LAST), (1, 0, False, SECOND)]
+
+    def pieces(flow, stage):
+        return [
+            (route, 3 * route + q, piece, sum(p[3] for p in group[:q]))
+            for route, group in enumerate(flow[3][stage])
+            for q, piece in enumerate(group)
+        ]
+
+    def part(buf, piece, shift, base):
+        kind, col, row, count = piece
+        if kind == "c":
+            return buf.at[col + shift, pl.ds(base + row, count)]
+        return buf.at[pl.ds(col + shift, count), base + row]
+
+    def to_relay(buf, flow, stage, route, index, piece, off):
+        return pltpu.make_async_remote_copy(
+            src_ref=part(buf, piece, 0, 8),
+            dst_ref=hold.at[stage, pl.ds(off, piece[3])],
+            send_sem=es.at[stage, index],
+            recv_sem=hr.at[stage, index % 3],
+            device_id=divmod(relays(flow[1])[route], width),
+            device_id_type=MESH,
+        )
+
+    def to_end(buf, flow, stage, index, piece, off):
+        shift, base = (-8, 0) if flow[2] else (8, 16)
+        return pltpu.make_async_remote_copy(
+            src_ref=hold.at[stage, pl.ds(off, piece[3])],
+            dst_ref=part(buf, piece, shift, base),
+            send_sem=hs.at[stage, index % 3],
+            recv_sem=er.at[stage, index],
+            device_id=divmod(flow[1], width),
+            device_id_type=MESH,
+        )
+
+    def edge_start(buf, stage, which, kinds):
+        flow = flows[which]
+
+        @pl.when(device == flow[0])
+        def _():
+            for route, index, piece, off in pieces(flow, stage):
+                if piece[0] in kinds:
+                    to_relay(buf, flow, stage, route, index, piece, off).start()
+
+    def edge_forward(buf, stage):
+        for flow in flows:
+            for k, relay in enumerate(relays(flow[1])):
+
+                @pl.when(device == relay)
+                def _():
+                    mine = [p for p in pieces(flow, stage) if p[0] == k]
+                    for route, index, piece, off in mine:
+                        to_relay(buf, flow, stage, route, index, piece, off).wait_recv()
+                        to_end(buf, flow, stage, index, piece, off).start()
+
+    def edge_receive(buf, stage, which):
+        flow = flows[which]
+
+        @pl.when(device == flow[1])
+        def _():
+            for route, index, piece, off in pieces(flow, stage):
+                to_end(buf, flow, stage, index, piece, off).wait_recv()
+
+    def edge_drain(buf, stage):
+        for flow in flows:
+
+            @pl.when(device == flow[0])
+            def _():
+                for route, index, piece, off in pieces(flow, stage):
+                    to_relay(buf, flow, stage, route, index, piece, off).wait_send()
+
+            for k, relay in enumerate(relays(flow[1])):
+
+                @pl.when(device == relay)
+                def _():
+                    for route, index, piece, off in pieces(flow, stage):
+                        if route == k:
+                            to_end(buf, flow, stage, index, piece, off).wait_send()
+
     barrier = pltpu.get_barrier_semaphore()
+    extra = jnp.int32(0)
+    for flow in flows:
+        extra = extra + jnp.where(device == flow[0], 2, 0)
+        for relay in relays(flow[1])[2:]:
+            extra = extra + jnp.where(device == relay, 1, 0)
+
+            @pl.when(device == relay)
+            def _():
+                pl.semaphore_signal(
+                    barrier, inc=1, device_id=divmod(flow[0], width), device_id_type=MESH
+                )
+
+            @pl.when(device == flow[1])
+            def _():
+                pl.semaphore_signal(
+                    barrier, inc=1, device_id=divmod(relay, width), device_id_type=MESH
+                )
+
     for o in OFFSETS:
         pl.semaphore_signal(barrier, inc=1, device_id=(mesh_row, peer(o)), device_id_type=MESH)
 
@@ -154,37 +286,6 @@
             for u in range(7, -1, -1)
         ]
 
-    def apart(buf, first_col, cols, row, to_col, to_row, ssem, rsem, dev):
-        return pltpu.make_async_remote_copy(
-            src_ref=buf.at[pl.ds(first_col, cols), row],
-            dst_ref=buf.at[pl.ds(to_col, cols), to_row],
-            send_sem=ssem,
-            recv_sem=rsem,
-            device_id=place(dev),
-            device_id_type=MESH,
-        )
-
-    def edge_first(buf, ss, rs):
-        return [
-            send(buf, 16 + u, 0, u + 1, 8 + u, 0, ss.at[u], rs.at[u], device + 1)
-            for u in range(8)
-        ]
-
-    def edge_first_row(buf, ss, rs):
-        return [apart(buf, 8, 8, 8, 0, 0, ss.at[8], rs.at[8], device + 1)]
-
-    def edge_last(buf, ss, rs):
-        return [
-            send(buf, u, u + 1, 7 - u, 8 + u, 17 + u, ss.at[u], rs.at[u], device - 1)
-            for u in range(7)
-        ]
-
-    def edge_second(buf, ss, rs):
-        return [send(buf, 15, 0, 8, 23, 16, ss.at[0], rs.at[0], device - 1)]
-
-    def edge_second_row(buf, ss, rs):
-        return [apart(buf, 8, 7, 15, 16, 23, ss.at[8], rs.at[8], device - 1)]
-
     def start_all(copies):
         for copy in copies:
             copy.start()
@@ -193,13 +294,8 @@
         copy.wait()
     pack(table, 0, orth, win, 8)
 
-    @pl.when(has_low & has_high)
-    def _():
-        pl.semaphore_wait(barrier, width + 1)
-
-    @pl.when(jnp.logical_not(has_low & has_high))
-    def _():
-        pl.semaphore_wait(barrier, width)
+    neighbours = has_low.astype(jnp.int32) + has_high.astype(jnp.int32)
+    pl.semaphore_wait(barrier, width - 1 + neighbours + extra)
 
     @pl.when(has_high)
     def _():
@@ -209,10 +305,8 @@
     def _():
         start_all([down_col(win, col, zds, zdr, 1) for col in range(14, 7, -1)])
 
-    @pl.when(device == 1)
-    def _():
-        start_all(edge_second(win, ezs, ezr) + edge_second_row(win, ezs, ezr))
-
+    for which in range(3):
+        edge_start(win, 0, which, "cr")
     zero_window(pwin, 0, 0)
 
     def clear(q, carry):
@@ -239,19 +333,11 @@
     def _():
         start_all(down_tri(win, zds, zdr))
 
-    @pl.when(is_first)
-    def _():
-        start_all(edge_first(win, ezs, ezr))
-
-    @pl.when(is_last)
-    def _():
-        start_all(edge_last(win, ezs, ezr))
-
     for copy in floads:
         copy.wait()
     pack(table, 1, turned, left, 0)
 
-    def outer(lhs, buf, us, ur, ds, dr, es, er, put, second):
+    def outer(lhs, buf, us, ur, ds, dr, put, second):
         skip_up, skip_down = (1, 0) if second else (0, 1)
 
         def one(q, carry):
@@ -274,21 +360,15 @@
             def _():
                 down_col(buf, 2 * pair - 7, ds, dr, skip_down).wait_recv()
 
-            if second:
-
-                @pl.when((q == 0) & (device == 1))
+            @pl.when(pair == 11)
+            def _():
+                edge_receive(buf, int(second), 2)
+
+            if not second:
+
+                @pl.when(q == 2)
                 def _():
-                    edge_first_row(buf, es, er)[0].wait_recv()
-
-                @pl.when((pair == 11) & is_first)
-                def _():
-                    edge_second(buf, es, er)[0].wait_recv()
-            else:
-
-                @pl.when((pair == 11) & is_first)
-                def _():
-                    edge_second(buf, es, er)[0].wait_recv()
-                    edge_second_row(buf, es, er)[0].wait_recv()
+                    edge_forward(buf, 0)
 
             low = jnp.where(pair < 4, 0, pair - 8)
             low = jnp.where(is_first, jnp.where(pair < 4, 4, 0), low)
@@ -304,7 +384,7 @@
 
         lax.fori_loop(0, 8, one, 0)
 
-    def wait_middle(buf, us, ur, ds, dr, es, er):
+    def wait_middle(buf, us, ur, ds, dr, stage):
         @pl.when(has_low)
         def _():
             for copy in up_tri(buf, us, ur):
@@ -315,15 +395,8 @@
             for copy in down_tri(buf, ds, dr):
                 copy.wait_recv()
 
-        @pl.when(device == 1)
-        def _():
-            for copy in edge_first(buf, es, er):
-                copy.wait_recv()
-
-        @pl.when(device == last - 1)
-        def _():
-            for copy in edge_last(buf, es, er):
-                copy.wait_recv()
+        edge_receive(buf, stage, 0)
+        edge_receive(buf, stage, 1)
 
     def middle(lhs, buf, put, after):
         def one(q, carry):
@@ -353,7 +426,7 @@
     def put_product(col, row, value):
         pwin[col, 8 + row] = jnp.where(table[2, col, row] >= 0, value, 0.0).astype(BF)
 
-    outer(left, win, zus, zur, zds, zdr, ezs, ezr, put_product, False)
+    outer(left, win, zus, zur, zds, zdr, put_product, False)
 
     @pl.when(has_high)
     def _():
@@ -363,15 +436,10 @@
     def _():
         start_all(down_tri(pwin, pds, pdr))
 
-    wait_middle(win, zus, zur, zds, zdr, ezs, ezr)
-
-    @pl.when(is_first)
-    def _():
-        start_all(edge_first(pwin, eps, epr))
-
-    @pl.when(is_last)
-    def _():
-        start_all(edge_last(pwin, eps, epr))
+    wait_middle(win, zus, zur, zds, zdr, 0)
+
+    edge_start(pwin, 1, 0, "c")
+    edge_start(pwin, 1, 1, "c")
 
     def send_up(pair):
         @pl.when(has_high)
@@ -391,10 +459,7 @@
         @pl.when(q == 1)
         def _():
             send_up(7)
-
-            @pl.when(device == 1)
-            def _():
-                start_all(edge_second(pwin, eps, epr))
+            edge_start(pwin, 1, 2, "c")
 
         @pl.when(q == 2)
         def _():
@@ -418,20 +483,18 @@
     send_down(6)
     send_down(7)
 
-    @pl.when(is_first)
-    def _():
-        start_all(edge_first_row(pwin, eps, epr))
-
+    edge_start(pwin, 1, 0, "r")
     lax.fori_loop(2, C, turn, 0)
+    edge_forward(pwin, 1)
 
     def put_orth(col, row, value):
         orth[col, row] = value.astype(BF)
 
-    wait_middle(pwin, pus, pur, pds, pdr, eps, epr)
+    wait_middle(pwin, pus, pur, pds, pdr, 1)
     middle(turned, pwin, put_orth, lambda q: None)
-    outer(turned, pwin, pus, pur, pds, pdr, eps, epr, put_orth, True)
-
-    def wait_sends(buf, us, ur, ds, dr, es, er, product):
+    outer(turned, pwin, pus, pur, pds, pdr, put_orth, True)
+
+    def wait_sends(buf, us, ur, ds, dr, product):
         def drain(copies):
             for copy in copies:
                 copy.wait_send()
@@ -446,21 +509,7 @@
             drain([down_col(buf, col, ds, dr, 1 - product) for col in range(8, 15)])
             drain(down_tri(buf, ds, dr))
 
-        @pl.when(is_first)
-        def _():
-            drain(edge_first(buf, es, er))
-            if product:
-                drain(edge_first_row(buf, es, er))
-
-        @pl.when(device == 1)
-        def _():
-            drain(edge_second(buf, es, er))
-            if not product:
-                drain(edge_second_row(buf, es, er))
-
-        @pl.when(is_last)
-        def _():
-            drain(edge_last(buf, es, er))
+        edge_drain(buf, product)
 
     def stage(e):
         row = jnp.int32(0)
@@ -470,31 +519,37 @@
         for s in range(K):
             win[e, s] = orth[rel[3, row, s], row]
 
-    wait_sends(win, zus, zur, zds, zdr, ezs, ezr, 0)
-
-    packets = []
-    for q, o in enumerate(OFFSETS):
-        stage(peer(o))
-        packets.append(
-            pltpu.make_async_remote_copy(
-                src_ref=win.at[peer(o), pl.ds(0, K)],
-                dst_ref=incoming.at[mesh_col],
-                send_sem=xs.at[q],
-                recv_sem=xr.at[q],
-                device_id=(mesh_row, peer(o)),
-                device_id_type=MESH,
-            )
+    wait_sends(win, zus, zur, zds, zdr, 0)
+
+    def packet(q, p):
+        there = peer(OFFSETS[q])
+        slots = pl.ds(p * K // PARTS, K // PARTS)
+        return pltpu.make_async_remote_copy(
+            src_ref=win.at[there, slots],
+            dst_ref=incoming.at[mesh_col, slots],
+            send_sem=xs.at[p, q],
+            recv_sem=xr.at[p, q],
+            device_id=(mesh_row, there),
+            device_id_type=MESH,
         )
+
+    count = width - 1
+    for q in range(count):
+        stage(peer(OFFSETS[q]))
         if q:
-            packets[q - 1].start()
+            packet(q - 1, 0).start()
     stage(mesh_col)
-    packets[-1].start()
+    packet(count - 1, 0).start()
+    for p in range(1, PARTS):
+        for q in range(count):
+            packet(q, p).start()
     mine = pltpu.make_async_copy(win.at[mesh_col, pl.ds(0, K)], incoming.at[mesh_col], sem_o)
     mine.start()
-    wait_sends(pwin, pus, pur, pds, pdr, eps, epr, 1)
+    wait_sends(pwin, pus, pur, pds, pdr, 1)
     mine.wait()
-    for packet in packets:
-        packet.wait()
+    for p in range(PARTS):
+        for q in range(count):
+            packet(q, p).wait()
 
 
 def take_kernel(width, new_index, incoming, out, held, sem_in, sem_out):
@@ -555,8 +610,10 @@
             dma,
         ]
         + [dma((15,))] * 8
-        + [dma((9,))] * 4
-        + [dma((width - 1,))] * 2,
+        + [pltpu.VMEM((2, HOLD, T, T), BF)]
+        + [dma((2, 3 * ROUTES))] * 2
+        + [dma((2, 3))] * 2
+        + [dma((PARTS, width - 1))] * 2,
         compiler_params=pltpu.CompilerParams(
             vmem_limit_bytes=VMEM_LIMIT, collective_id=0, has_side_effects=True
         ),

time: 285 us -> 265 us (0.930)
  the two profiles are of different devices: /device:TPU:100 before, /device:TPU:124 now
where the time goes in v4:
time: 265 us
  Pallas kernels  262 us (99%)
    pallas_call x1, Pallas kernels, body(): pl.pallas_call(functools.partial(fused_kernel, last, width, 4), out_shape...  257 us

profile of v4, /device:TPU:124, one launch (start us, length us, event | category | flops | bytes accessed | tf_op | source)
XLA Modules:
  0.0 265.1 jit_solution(16641215148770813753)
XLA Ops:
  0.0 0.8 constant_dynamic-slice_fusion.2
  0.8 0.1 copy.26
  0.9 0.1 copy.25
  0.9 0.8 constant_dynamic-slice_fusion
  1.7 0.1 copy.28
  1.8 0.1 copy.27
  1.9 0.0 copy-start
  1.9 0.1 copy.22
  2.0 0.1 select_reduce_fusion
  2.2 0.1 copy.23
  2.2 0.6 broadcast_add_fusion.table
  2.9 0.0 copy-done
  2.9 257.5 %fused.1.incoming = bf16[16,15,128,128]{3,2,1,0:T(8,128)(2,1)} custom-call(s32[3,24,8]{2,1,0:T(8,128)} %broadcast_add_fusion.table, s32[4,8,15]{2,1,0:T(8,128)} %copy-done, s32[1024]{0:T(1024)} %new_index.3, bf16[8,15,128,128]{3,2,1,0:T(8,128)(2,1)} %z.1, bf16[8,15,128,128]{3,2,1,0:T(8,128)(2,1)} %f.1), custom_call_target="tpu_custom_call" | custom-call | tf_op jit(solution)/shard_map/fused/pallas_call | solution.py:597
  260.3 4.7 %take.1 = bf16[8,15,128,128]{3,2,1,0:T(8,128)(2,1)} custom-call(s32[1024]{0:T(1024)} %new_index.3, bf16[16,15,128,128]{3,2,1,0:T(8,128)(2,1)} %fused.1.incoming), custom_call_target="tpu_custom_call" | custom-call | tf_op jit(solution)/shard_map/take/pallas_call | solution.py:622
  (3 shorter events, 0.0 us)
Async XLA Ops:
  1.9 1.0 copy-start

commit v5 on v4

--- a/solution.py
+++ b/solution.py
@@ -24,7 +24,7 @@
 )
 
 
-PARTS = 3
+PARTS = 5
 ROUTES = 4
 FIRST = (
     tuple((("c", 23 - k, 0, 8 - k), ("c", 16 + k, 0, k + 1)) for k in range(ROUTES)),
@@ -72,7 +72,7 @@
     lax.fori_loop(0, 16, one, 0)
 
 
-def pack(table, which, raw, dst, base):
+def pack(table, which, raw, dst, base, first, end):
     def one(col, carry):
         for t in range(R):
             slot = table[which, col, t]
@@ -80,7 +80,7 @@
             dst[col, base + t] = jnp.where(slot >= 0, tile, jnp.zeros_like(tile))
         return carry
 
-    lax.fori_loop(0, C, one, 0)
+    lax.fori_loop(first, end, one, 0)
 
 
 def band_step(left, win, pair, rows, start, depth, put):
@@ -99,7 +99,7 @@
 def fused_kernel(
     last, width, side, table, rel, new_index, z, f, incoming,
     win, pwin, left, turned, orth, sem_z, sem_f, sem_o,
-    zus, zur, zds, zdr, pus, pur, pds, pdr, hold, es, er, hs, hr, xs, xr,
+    zus, zur, zds, zdr, pus, pur, pds, pdr, hold, es, er, hs, hr, xs, xr, ready,
 ):
     mesh_row = lax.axis_index("row")
     mesh_col = lax.axis_index("col")
@@ -116,7 +116,7 @@
     floads = [
         pltpu.make_async_copy(f.at[t], turned.at[pl.ds(0, K), t], sem_f.at[t]) for t in range(R)
     ]
-    for copy in loads + floads:
+    for copy in loads:
         copy.start()
 
     def place(dev):
@@ -292,7 +292,9 @@
 
     for copy in loads:
         copy.wait()
-    pack(table, 0, orth, win, 8)
+    for copy in floads:
+        copy.start()
+    pack(table, 0, orth, win, 8, 8, 16)
 
     neighbours = has_low.astype(jnp.int32) + has_high.astype(jnp.int32)
     pl.semaphore_wait(barrier, width - 1 + neighbours + extra)
@@ -305,8 +307,11 @@
     def _():
         start_all([down_col(win, col, zds, zdr, 1) for col in range(14, 7, -1)])
 
+    pack(table, 0, orth, win, 8, 0, 8)
+    pack(table, 0, orth, win, 8, 16, C)
     for which in range(3):
         edge_start(win, 0, which, "cr")
+
     zero_window(pwin, 0, 0)
 
     def clear(q, carry):
@@ -335,7 +340,7 @@
 
     for copy in floads:
         copy.wait()
-    pack(table, 1, turned, left, 0)
+    pack(table, 1, turned, left, 0, 0, C)
 
     def outer(lhs, buf, us, ur, ds, dr, put, second):
         skip_up, skip_down = (1, 0) if second else (0, 1)
@@ -534,13 +539,13 @@
         )
 
     count = width - 1
+    for o in OFFSETS:
+        pl.semaphore_signal(ready, inc=1, device_id=(mesh_row, peer(o)), device_id_type=MESH)
     for q in range(count):
         stage(peer(OFFSETS[q]))
-        if q:
-            packet(q - 1, 0).start()
     stage(mesh_col)
-    packet(count - 1, 0).start()
-    for p in range(1, PARTS):
+    pl.semaphore_wait(ready, count)
+    for p in range(PARTS):
         for q in range(count):
             packet(q, p).start()
     mine = pltpu.make_async_copy(win.at[mesh_col, pl.ds(0, K)], incoming.at[mesh_col], sem_o)
@@ -613,7 +618,8 @@
         + [pltpu.VMEM((2, HOLD, T, T), BF)]
         + [dma((2, 3 * ROUTES))] * 2
         + [dma((2, 3))] * 2
-        + [dma((PARTS, width - 1))] * 2,
+        + [dma((PARTS, width - 1))] * 2
+        + [pltpu.SemaphoreType.REGULAR],
         compiler_params=pltpu.CompilerParams(
             vmem_limit_bytes=VMEM_LIMIT, collective_id=0, has_side_effects=True
         ),

time: 265 us -> 244 us (0.921)
  the two profiles are of different devices: /device:TPU:124 before, /device:TPU:8 now
where the time goes in v5:
time: 244 us
  Pallas kernels  241 us (99%)
    pallas_call x1, Pallas kernels, body(): pl.pallas_call(functools.partial(fused_kernel, last, width, 4), out_shape...  236 us

profile of v5, /device:TPU:8, one launch (start us, length us, event | category | flops | bytes accessed | tf_op | source)
XLA Modules:
  0.0 243.9 jit_solution(7603553174824819988)
XLA Ops:
  0.0 0.8 constant_dynamic-slice_fusion.2
  0.8 0.1 copy.26
  0.9 0.1 copy.25
  0.9 0.9 constant_dynamic-slice_fusion
  1.8 0.1 copy.28
  1.9 0.1 copy.27
  2.0 0.0 copy-start
  2.0 0.1 copy.22
  2.1 0.1 select_reduce_fusion
  2.2 0.1 copy.23
  2.3 0.6 broadcast_add_fusion.table
  2.9 0.0 copy-done
  2.9 236.3 %fused.1.incoming = bf16[16,15,128,128]{3,2,1,0:T(8,128)(2,1)} custom-call(s32[3,24,8]{2,1,0:T(8,128)} %broadcast_add_fusion.table, s32[4,8,15]{2,1,0:T(8,128)} %copy-done, s32[1024]{0:T(1024)} %new_index.3, bf16[8,15,128,128]{3,2,1,0:T(8,128)(2,1)} %z.1, bf16[8,15,128,128]{3,2,1,0:T(8,128)(2,1)} %f.1), custom_call_target="tpu_custom_call" | custom-call | tf_op jit(solution)/shard_map/fused/pallas_call | solution.py:602
  239.2 4.7 %take.1 = bf16[8,15,128,128]{3,2,1,0:T(8,128)(2,1)} custom-call(s32[1024]{0:T(1024)} %new_index.3, bf16[16,15,128,128]{3,2,1,0:T(8,128)(2,1)} %fused.1.incoming), custom_call_target="tpu_custom_call" | custom-call | tf_op jit(solution)/shard_map/take/pallas_call | solution.py:628
  (3 shorter events, 0.0 us)
Async XLA Ops:
  2.0 1.0 copy-start

commit v6 on v5

--- a/solution.py
+++ b/solution.py
@@ -72,10 +72,10 @@
     lax.fori_loop(0, 16, one, 0)
 
 
-def pack(table, which, raw, dst, base, first, end):
+def pack(table, line, lane, raw, dst, base, first, end):
     def one(col, carry):
         for t in range(R):
-            slot = table[which, col, t]
+            slot = table[line + col, lane + t]
             tile = raw[jnp.maximum(slot, 0), t]
             dst[col, base + t] = jnp.where(slot >= 0, tile, jnp.zeros_like(tile))
         return carry
@@ -97,9 +97,10 @@
 
 
 def fused_kernel(
-    last, width, side, table, rel, new_index, z, f, incoming,
+    last, width, side, new_index, zpat, fpat, ppat, rpat, z, f, incoming,
     win, pwin, left, turned, orth, sem_z, sem_f, sem_o,
     zus, zur, zds, zdr, pus, pur, pds, pdr, hold, es, er, hs, hr, xs, xr, ready,
+    pats, lines, table, sem_p, sem_t,
 ):
     mesh_row = lax.axis_index("row")
     mesh_col = lax.axis_index("col")
@@ -110,6 +111,14 @@
     is_first = device == 0
     is_last = device == last
 
+    lane = mesh_col * R
+    group = pl.multiple_of(mesh_row * width * R, width * R)
+    pat_loads = [
+        pltpu.make_async_copy(pat.at[:, pl.ds(group, width * R)], pats.at[k], sem_p.at[k])
+        for k, pat in enumerate((zpat, fpat, ppat, rpat))
+    ]
+    for copy in pat_loads:
+        copy.start()
     loads = [
         pltpu.make_async_copy(z.at[t], orth.at[pl.ds(0, K), t], sem_z.at[t]) for t in range(R)
     ]
@@ -240,6 +249,19 @@
 
     zero_window(win, 16, 23)
 
+    for copy in pat_loads:
+        copy.wait()
+    slot_ids = lax.broadcasted_iota(jnp.int32, (K, width * R), 0)
+    for k in range(3):
+        for col in range(C):
+            hit = pats[k] == device * R + (col - 8)
+            lines[k * C + col] = jnp.max(jnp.where(hit, slot_ids, -1), axis=0)
+    lines[pl.ds(3 * C + 8, 8)] = jnp.zeros((8, width * R), jnp.int32)
+    there = jnp.clip(pats[3] - (device * R - 8), 0, C)
+    lines[pl.ds(3 * C, K)] = jnp.where(pats[3] >= 0, there, C)
+    to_scalars = pltpu.make_async_copy(lines, table, sem_t)
+    to_scalars.start()
+
     @pl.when(is_first)
     def _():
         zero_side(win, 0, 0)
@@ -290,11 +312,12 @@
         for copy in copies:
             copy.start()
 
+    to_scalars.wait()
     for copy in loads:
         copy.wait()
     for copy in floads:
         copy.start()
-    pack(table, 0, orth, win, 8, 8, 16)
+    pack(table, 0, lane, orth, win, 8, 8, 16)
 
     neighbours = has_low.astype(jnp.int32) + has_high.astype(jnp.int32)
     pl.semaphore_wait(barrier, width - 1 + neighbours + extra)
@@ -307,8 +330,8 @@
     def _():
         start_all([down_col(win, col, zds, zdr, 1) for col in range(14, 7, -1)])
 
-    pack(table, 0, orth, win, 8, 0, 8)
-    pack(table, 0, orth, win, 8, 16, C)
+    pack(table, 0, lane, orth, win, 8, 0, 8)
+    pack(table, 0, lane, orth, win, 8, 16, C)
     for which in range(3):
         edge_start(win, 0, which, "cr")
 
@@ -340,7 +363,7 @@
 
     for copy in floads:
         copy.wait()
-    pack(table, 1, turned, left, 0, 0, C)
+    pack(table, C, lane, turned, left, 0, 0, C)
 
     def outer(lhs, buf, us, ur, ds, dr, put, second):
         skip_up, skip_down = (1, 0) if second else (0, 1)
@@ -429,7 +452,7 @@
         lax.fori_loop(0, 4, one, 0)
 
     def put_product(col, row, value):
-        pwin[col, 8 + row] = jnp.where(table[2, col, row] >= 0, value, 0.0).astype(BF)
+        pwin[col, 8 + row] = jnp.where(table[2 * C + col, lane + row] >= 0, value, 0.0).astype(BF)
 
     outer(left, win, zus, zur, zds, zdr, put_product, False)
 
@@ -522,7 +545,7 @@
             there = lax.rem(new_index[device * R + t] // R, width)
             row = jnp.where(there == e, t, row)
         for s in range(K):
-            win[e, s] = orth[rel[3, row, s], row]
+            win[e, s] = orth[table[3 * C + s, lane + row], row]
 
     wait_sends(win, zus, zur, zds, zdr, 0)
 
@@ -585,24 +608,11 @@
 ):
     width = lax.axis_size("col")
     last = lax.axis_size("row") * width - 1
-    device = lax.axis_index(("row", "col"))
-    first_row = device * R
-
-    def own(pattern):
-        return lax.dynamic_slice_in_dim(pattern, first_row, R, 0)
-
-    rel = jnp.stack(
-        [own(basis_pattern), own(fock_pattern), own(product_pattern), own(result_pattern)]
-    )
-    rel = jnp.where(rel >= 0, rel - first_row + 8, C)
-    cols = jnp.arange(C, dtype=jnp.int32)[None, :, None, None]
-    slots = jnp.arange(1, K + 1, dtype=jnp.int32)
-    table = jnp.sum(jnp.where(rel[:3, None] == cols, slots, 0), axis=-1) - 1
     dma = pltpu.SemaphoreType.DMA
     incoming = pl.pallas_call(
         functools.partial(fused_kernel, last, width, 4),
         out_shape=jax.ShapeDtypeStruct((width, K, T, T), BF),
-        in_specs=[SMEM] * 3 + [ANY] * 2,
+        in_specs=[SMEM] + [ANY] * 6,
         out_specs=ANY,
         scratch_shapes=[
             pltpu.VMEM((C, C, T, T), BF),
@@ -619,12 +629,24 @@
         + [dma((2, 3 * ROUTES))] * 2
         + [dma((2, 3))] * 2
         + [dma((PARTS, width - 1))] * 2
-        + [pltpu.SemaphoreType.REGULAR],
+        + [pltpu.SemaphoreType.REGULAR]
+        + [pltpu.VMEM((4, K, width * R), jnp.int32)]
+        + [pltpu.VMEM((3 * C + 16, width * R), jnp.int32)]
+        + [pltpu.SMEM((3 * C + 16, width * R), jnp.int32)]
+        + [dma((4,)), dma],
         compiler_params=pltpu.CompilerParams(
             vmem_limit_bytes=VMEM_LIMIT, collective_id=0, has_side_effects=True
         ),
         name="fused",
-    )(table, rel, new_index, basis_tiles, fock_tiles)
+    )(
+        new_index,
+        basis_pattern.T,
+        fock_pattern.T,
+        product_pattern.T,
+        result_pattern.T,
+        basis_tiles,
+        fock_tiles,
+    )
     return pl.pallas_call(
         functools.partial(take_kernel, width),
         out_shape=jax.ShapeDtypeStruct((R, K, T, T), BF),

time: 244 us -> 241 us (0.988)
  no operation moved by 1% of the time
where the time goes in v6:
time: 241 us
  Pallas kernels  241 us (100%)
    pallas_call x1, Pallas kernels, body(): pl.pallas_call(functools.partial(fused_kernel, last, width, 4), out_shape...  236 us

profile of v6, /device:TPU:8, one launch (start us, length us, event | category | flops | bytes accessed | tf_op | source)
XLA Modules:
  0.0 241.1 jit_solution(6870043140884991072)
XLA Ops:
  0.0 236.3 %fused.1.incoming = bf16[16,15,128,128]{3,2,1,0:T(8,128)(2,1)} custom-call(s32[1024]{0:T(1024)} %new_index.3, s32[15,1024]{1,0:T(8,128)} %bitcast.4, s32[15,1024]{1,0:T(8,128)} %bitcast.5, s32[15,1024]{1,0:T(8,128)} %bitcast.6, s32[15,1024]{1,0:T(8,128)} %bitcast.7, bf16[8,15,128,128]{3,2,1,0:T(8,128)(2,1)} %z.1, bf16[8,15,128,128]{3,2,1,0:T(8,128)(2,1)} %f.1), custom_call_target="tpu_custom_call" | custom-call | tf_op jit(solution)/shard_map/fused/pallas_call | solution.py:612
  236.3 4.7 %take.1 = bf16[8,15,128,128]{3,2,1,0:T(8,128)(2,1)} custom-call(s32[1024]{0:T(1024)} %new_index.3, bf16[16,15,128,128]{3,2,1,0:T(8,128)(2,1)} %fused.1.incoming), custom_call_target="tpu_custom_call" | custom-call | tf_op jit(solution)/shard_map/take/pallas_call | solution.py:650
